TPU v7x, 128 devices: a whole 4x4x4 slice. The times are simulated.
128 devices in a mesh: grp: 4 (over z), sfc: 32 (over y, x, core).
Axes of the slice: x: 4, y: 4, z: 4, core: 2. Of those that a mesh axis runs over, the one named last changes fastest.
Arguments:
- coarse_state: float32 [384, 5, 32, 1024], P(('grp', 'sfc')), may hold values from -6 to 6
- fine_old: float32 [1280, 5, 32, 1024], P(('grp', 'sfc')), may hold values from -6 to 6
- coarse_owner: int32 [256], replicated, may hold values from 0 to 127, as said below
- fine_owner_old: int32 [1024], replicated, may hold values from 0 to 127, as said below
- fine_owner_new: int32 [1024], replicated, may hold values from 0 to 127, as said below
- fine_nbr: int32 [1024, 6], replicated, may hold values from -1 to 1023, as said below
- reflux_map: int32 [1024, 3], replicated, may hold values from -1 to 254, as said below
Outputs:
- coarse_out: float32 [384, 5, 32, 1024], P(('grp', 'sfc'))
- fine_new: float32 [1792, 5, 32, 1024], P(('grp', 'sfc'))
Inputs may be any that keep to these rules, and one draw needn't show every extreme that they name: `coarse_owner`: Non-decreasing; each device holds 1 to 3 coarse patches, and some device holds 3. `fine_owner_old`: Non-decreasing; each device holds 6 to 10 fine patches. `fine_owner_new`: Non-decreasing; each device holds 3 to 14 fine patches. Along the index over grp and sfc together, each patch's new owner is its old owner or the device next to it, and at most 2 patches go from one device to each side. The owners of a fine patch, of its neighbours and of its reflux target's coarse patch are at most two devices apart. `fine_nbr`: patches 8k to 8k + 7 refine coarse patch 2k + 1 as a 2 x 2 x 2 block in an order drawn per block; y and z neighbours are the other patch of the block in that direction (both faces), the x neighbour inside the block is given on the inner face and -1 on the outer one. `reflux_map`: Columns: the coarse patch beyond the block across the patch's outer x face (2k or 2k + 2, -1 beyond the domain), that coarse patch's face (0 lower x, 1 upper x), and the quarter 2 * (y half) + (z half) covered. Every quarter is covered by exactly one fine patch.
All inputs are finite; a program needn't handle non-finite values.
Results may differ from a plain program's by a relative error of at most 0.00005.
Values sent between devices are 32-bit elements; how exact they have to be, the bound alone decides.
A program may use at most 256 MiB of HBM per device.

v0:
```python
import jax
import jax.numpy as jnp
from jax import lax
from jax.sharding import PartitionSpec as P

FNEW = 14


background = (0.6, -0.4, 0.25)
signal = (1.8, 1.6, 1.45)
sound_sq = 1.44
courant = 0.2
opposite = (1, 0, 3, 2, 5, 4)


def shifted(block, axis, distance):
    devices = range(lax.axis_size(axis))
    route = [(i - distance, i) for i in devices if i - distance in devices]
    return lax.ppermute(block, axis, route)


def face_flux(left_q, right_q, direction):
    total_q = left_q + right_q
    jump_q = right_q - left_q
    speed_a = background[direction]
    normal = total_q[1 + direction]
    pieces = [speed_a * total_q[0] + normal]
    for component in range(3):
        entry_q = speed_a * total_q[1 + component]
        if component == direction:
            entry_q = entry_q + total_q[4]
        pieces.append(entry_q)
    pieces.append(speed_a * total_q[4] + sound_sq * normal)
    return 0.5 * jnp.stack(pieces) - 0.5 * signal[direction] * jump_q


def lane_tables(edge_len):
    plane_len = edge_len * edge_len
    lanes = jnp.arange(plane_len, dtype=jnp.int32)[None, :]
    row_ids = jnp.arange(edge_len, dtype=jnp.int32)[:, None]
    place_first = (lanes == row_ids * edge_len).astype(jnp.float32)
    place_last = (lanes == row_ids * edge_len + edge_len - 1).astype(jnp.float32)
    return (place_first, place_last)


def pick_lanes(patch_state, place):
    fields, edge_len, plane_len = patch_state.shape
    picked = jnp.dot(
        patch_state.reshape(fields * edge_len, plane_len), place.T, precision=lax.Precision.HIGHEST
    )
    return picked.reshape(fields, edge_len, edge_len)


def spread_lanes(layer, place):
    fields, edge_len, other_len = layer.shape
    spread = jnp.dot(
        layer.reshape(fields * edge_len, other_len), place, precision=lax.Precision.HIGHEST
    )
    return spread.reshape(fields, edge_len, place.shape[1])


def boundary_layers(patch_state, place_first, place_last):
    fields, edge_len, plane_len = patch_state.shape
    lower_y = patch_state[:, :, :edge_len].reshape(fields, plane_len)
    upper_y = patch_state[:, :, plane_len - edge_len :].reshape(fields, plane_len)
    lower_z = pick_lanes(patch_state, place_first).reshape(fields, plane_len)
    upper_z = pick_lanes(patch_state, place_last).reshape(fields, plane_len)
    return jnp.stack([patch_state[:, 0], patch_state[:, -1], lower_y, upper_y, lower_z, upper_z])


def advance(patch_state, ghosts, place_first, place_last):
    fields, edge_len, plane_len = patch_state.shape
    lanes = jnp.arange(plane_len, dtype=jnp.int32)[None, None, :]
    z_pos = lanes % edge_len
    ext_x = jnp.concatenate([ghosts[0][:, None], patch_state, ghosts[1][:, None]], axis=1)
    flux_x = face_flux(ext_x[:, :-1], ext_x[:, 1:], 0)
    upper_ghost_y = jnp.pad(
        ghosts[3].reshape(fields, edge_len, edge_len), ((0, 0), (0, 0), (plane_len - edge_len, 0))
    )
    right_y = jnp.where(
        lanes >= plane_len - edge_len, upper_ghost_y, jnp.roll(patch_state, -edge_len, axis=2)
    )
    flux_up_y = face_flux(patch_state, right_y, 1)
    bottom_y = face_flux(
        ghosts[2].reshape(fields, edge_len, edge_len), patch_state[:, :, :edge_len], 1
    )
    bottom_y = jnp.pad(bottom_y, ((0, 0), (0, 0), (0, plane_len - edge_len)))
    flux_low_y = jnp.where(lanes < edge_len, bottom_y, jnp.roll(flux_up_y, edge_len, axis=2))
    upper_ghost_z = spread_lanes(ghosts[5].reshape(fields, edge_len, edge_len), place_last)
    right_z = jnp.where(z_pos == edge_len - 1, upper_ghost_z, jnp.roll(patch_state, -1, axis=2))
    flux_up_z = face_flux(patch_state, right_z, 2)
    first_z = pick_lanes(patch_state, place_first)
    bottom_z = spread_lanes(
        face_flux(ghosts[4].reshape(fields, edge_len, edge_len), first_z, 2), place_first
    )
    flux_low_z = jnp.where(z_pos == 0, bottom_z, jnp.roll(flux_up_z, 1, axis=2))
    change = flux_x[:, 1:] - flux_x[:, :-1] + (flux_up_y - flux_low_y) + (flux_up_z - flux_low_z)
    return (patch_state - courant * change, flux_x[:, 0], flux_x[:, -1])


def lookup(small_table, indices):
    hit_mask = indices[..., None] == jnp.arange(small_table.shape[0], dtype=jnp.int32)
    return jnp.sum(jnp.where(hit_mask, small_table, 0), axis=-1)


def body(
    coarse_state, fine_old, coarse_owner, fine_owner_old, fine_owner_new, fine_nbr, reflux_map
):
    coarse_cap, fields, edge_len, plane_len = coarse_state.shape
    old_cap = fine_old.shape[0]
    new_cap = FNEW
    half_edge = edge_len // 2
    coarse_total = coarse_owner.shape[0]
    devices = lax.axis_size(("grp", "sfc"))
    myself = lax.axis_index(("grp", "sfc"))
    place_first, place_last = lane_tables(edge_len)

    def layers_of(states):
        return jax.vmap(lambda one: boundary_layers(one, place_first, place_last))(states)

    def advance_all(states, ghosts):
        return jax.vmap(lambda one, sides: advance(one, sides, place_first, place_last))(
            states, ghosts
        )

    def range_starts(owners):
        device_marks = jnp.arange(devices + 1, dtype=jnp.int32)
        return jnp.sum((owners[None, :] < device_marks[:, None]).astype(jnp.int32), axis=1)

    old_start = range_starts(fine_owner_old)
    new_start = range_starts(fine_owner_new)
    coarse_start = range_starts(coarse_owner)
    old_base = old_start[myself]
    old_next = old_start[myself + 1]
    tail_pair = lax.dynamic_slice_in_dim(fine_old, old_next - old_base - 2, 2, 0)
    arrivals = []
    for shift_by, outgoing in ((1, tail_pair), (-1, fine_old[:2])):
        arrivals.append(shifted(outgoing, ("grp", "sfc"), shift_by))
    pooled = jnp.concatenate([fine_old, arrivals[0], arrivals[1]], axis=0)
    slot_ids = jnp.arange(new_cap, dtype=jnp.int32)
    new_base = new_start[myself]
    new_count = new_start[myself + 1] - new_base
    patch_ids = new_base + slot_ids
    live_slot = slot_ids < new_count
    take_rows = jnp.where(
        patch_ids < old_base,
        old_cap + patch_ids - old_base + 2,
        jnp.where(patch_ids >= old_next, old_cap + 2 + patch_ids - old_next, patch_ids - old_base),
    )
    take_rows = jnp.clip(take_rows, 0, old_cap + 3)
    moved_rows = jnp.take(pooled, take_rows, axis=0)
    states = jnp.where(live_slot[:, None, None, None], moved_rows, 0.0)
    window_one = 7
    window_two = 7
    face_plan = ((1, window_one), (2, window_two), (-1, window_one), (-2, window_two))
    neighbours = jnp.stack(
        [lookup(fine_nbr[:, face_num], patch_ids) for face_num in range(6)], axis=1
    )
    joined = (neighbours >= 0) & live_slot[:, None]
    nb_owner = lookup(fine_owner_new, neighbours)
    nb_start = lookup(new_start, nb_owner)
    nb_slot = neighbours - nb_start
    src_count = lookup(new_start, nb_owner + 1) - nb_start
    offset = nb_owner - myself
    slot_pos = jnp.where(
        offset == 0,
        nb_slot,
        jnp.where(
            offset == -1,
            new_cap + nb_slot - src_count + window_one,
            jnp.where(
                offset == -2,
                new_cap + window_one + nb_slot - src_count + window_two,
                jnp.where(
                    offset == 1,
                    new_cap + window_one + window_two + nb_slot,
                    new_cap + 2 * window_one + window_two + nb_slot,
                ),
            ),
        ),
    )
    face_ids = jnp.arange(6, dtype=jnp.int32)
    facing = jnp.array(opposite, dtype=jnp.int32)
    ghost_rows = jnp.where(
        joined, slot_pos * 6 + facing[None, :], slot_ids[:, None] * 6 + face_ids[None, :]
    )
    pool_slots = new_cap + 2 * window_one + 2 * window_two
    ghost_rows = jnp.clip(ghost_rows, 0, pool_slots * 6 - 1).reshape(-1)

    def fine_substep(current):
        layers = layers_of(current)
        padded = jnp.concatenate(
            [jnp.zeros((window_one,) + layers.shape[1:], jnp.float32), layers], axis=0
        )
        gathered = [layers]
        for shift_by, window in face_plan:
            if shift_by > 0:
                outgoing = lax.dynamic_slice_in_dim(
                    padded, new_count - window + window_one, window, 0
                )
            else:
                outgoing = layers[:window]
            gathered.append(shifted(outgoing, ("grp", "sfc"), shift_by))
        everything = jnp.concatenate(gathered, axis=0).reshape(-1, fields, plane_len)
        ghosts = jnp.take(everything, ghost_rows, axis=0).reshape(new_cap, 6, fields, plane_len)
        advanced, lower_flux, upper_flux = advance_all(current, ghosts)
        return (jnp.where(live_slot[:, None, None, None], advanced, 0.0), lower_flux, upper_flux)

    side_mine = lookup(reflux_map[:, 1], patch_ids)

    def register_rows(lower_flux, upper_flux):
        chosen = jnp.where((side_mine == 1)[:, None, None], lower_flux, upper_flux)
        summed = chosen.reshape(new_cap, fields, half_edge, 2, half_edge, 2).sum(axis=(3, 5))
        return summed.reshape(new_cap, fields * half_edge * half_edge)

    row_plan = (1, 2, -1, -2)

    def spread_rows(row_data):
        blocks = [row_data]
        for shift_by in row_plan:
            blocks.append(shifted(row_data, ("grp", "sfc"), shift_by))
        return jnp.concatenate(blocks, axis=0)

    sender_ids = myself - jnp.array((0,) + row_plan, dtype=jnp.int32)
    valid_sender = (sender_ids >= 0) & (sender_ids < devices)
    sender_clip = jnp.clip(sender_ids, 0, devices - 1)
    sender_base = lookup(new_start, sender_clip)
    sender_next = lookup(new_start, sender_clip + 1)
    row_patch = sender_base[:, None] + slot_ids[None, :]
    row_live = valid_sender[:, None] & (row_patch < sender_next[:, None])
    row_target = lookup(reflux_map[:, 0], row_patch)
    row_side = lookup(reflux_map[:, 1], row_patch)
    row_quarter = lookup(reflux_map[:, 2], row_patch)
    coarse_base = coarse_start[myself]
    coarse_count = coarse_start[myself + 1] - coarse_base
    coarse_slot = row_target - coarse_base
    row_valid = row_live & (row_target >= 0) & (coarse_slot >= 0) & (coarse_slot < coarse_count)
    row_key = jnp.where(row_valid, coarse_slot * 8 + row_side * 4 + row_quarter, -1).reshape(-1)
    selector = (jnp.arange(coarse_cap * 8, dtype=jnp.int32)[:, None] == row_key[None, :]).astype(
        jnp.float32
    )
    face_cover = selector.sum(axis=1).reshape(coarse_cap, 2, 4).max(axis=2)

    def collect(all_rows):
        return jnp.dot(selector, all_rows, precision=lax.Precision.HIGHEST)

    fine_one, lower_one, upper_one = fine_substep(states)
    register = collect(spread_rows(0.125 * register_rows(lower_one, upper_one)))
    fine_two, lower_two, upper_two = fine_substep(fine_one)
    register = register + collect(spread_rows(0.125 * register_rows(lower_two, upper_two)))
    coarse_layers = layers_of(coarse_state)
    last_upper = lax.dynamic_index_in_dim(coarse_layers, coarse_count - 1, 0, keepdims=False)[1]
    first_lower = coarse_layers[0, 0]
    edge_faces = []
    for shift_by, outgoing in ((1, last_upper), (-1, first_lower)):
        edge_faces.append(shifted(outgoing, ("grp", "sfc"), shift_by))
    coarse_slots = jnp.arange(coarse_cap, dtype=jnp.int32)
    global_ids = coarse_base + coarse_slots
    prev_upper = jnp.concatenate([edge_faces[0][None], coarse_layers[:-1, 1]], axis=0)
    next_lower = jnp.concatenate([coarse_layers[1:, 0], edge_faces[1][None]], axis=0)
    domain_start = ((coarse_slots == 0) & (coarse_base == 0))[:, None, None]
    lower_ghost = jnp.where(domain_start, coarse_layers[:, 0], prev_upper)
    at_end = (coarse_slots == coarse_count - 1)[:, None, None]
    domain_end = (global_ids == coarse_total - 1)[:, None, None]
    upper_ghost = jnp.where(
        at_end, jnp.where(domain_end, coarse_layers[:, 1], edge_faces[1][None]), next_lower
    )
    coarse_ghosts = jnp.stack(
        [
            lower_ghost,
            upper_ghost,
            coarse_layers[:, 3],
            coarse_layers[:, 2],
            coarse_layers[:, 5],
            coarse_layers[:, 4],
        ],
        axis=1,
    )
    coarse_new, coarse_lo, coarse_hi = advance_all(coarse_state, coarse_ghosts)
    face_reg = (
        register.reshape(coarse_cap, 2, 2, 2, fields, half_edge, half_edge)
        .transpose(0, 1, 4, 2, 5, 3, 6)
        .reshape(coarse_cap, 2, fields, plane_len)
    )
    coarse_new = coarse_new.at[:, :, 0].add(
        courant * face_cover[:, 0, None, None] * (face_reg[:, 0] - coarse_lo)
    )
    coarse_new = coarse_new.at[:, :, -1].add(
        -(courant * face_cover[:, 1, None, None] * (face_reg[:, 1] - coarse_hi))
    )
    coarse_live = (coarse_slots < coarse_count)[:, None, None, None]
    coarse_out = jnp.where(coarse_live, coarse_new, 0.0)
    return (coarse_out, fine_two)


def solution(mesh):
    placed = (
        P(("grp", "sfc"), None, None, None),
        P(("grp", "sfc"), None, None, None),
        P(),
        P(),
        P(),
        P(),
        P(),
    )
    return jax.shard_map(
        body,
        mesh=mesh,
        in_specs=placed,
        out_specs=(P(("grp", "sfc"), None, None, None), P(("grp", "sfc"), None, None, None)),
        check_vma=False,
    )
```

profile of v0, /device:TPU:96, one launch (start us, length us, event | category | flops | bytes accessed | tf_op | source)
XLA Modules:
  0.0 755.7 jit_solution(11856422258596103749)
XLA Ops:
  28.5 7.9 %collective-permute-start.3 = (f32[2,5,32,1024]{3,2,1,0:T(8,128)}, f32[2,5,32,1024]{3,2,1,0:T(8,128)}, u32[]{:S(2)}, u32[]{:S(2)}) collective-permute-start(f32[2,5,32,1024]{3,2,1,0:T(8,128)} %get-tuple-element.62), channel_id=1, source_target_pairs={{1,0},{2,1},{3,2},{4,3},{5,4},{6,5},{7,6},{8,7},{9,8},{10,9},{11,1... | collective-permute-start | bytes 3932168 | tf_op jit(solution)/shard_map/ppermute | solution.py:19
  120.1 9.8 %pad_maximum_fusion.4 = f32[14,5,32,1024]{3,2,1,0:T(8,128)} fusion(f32[2,5,32,1024]{3,2,1,0:T(8,128)} %collective-permute-done.3, f32[2,5,32,1024]{3,2,1,0:T(8,128)} %collective-permute-done.2, f32[10,5,32,1024]{3,2,1,0:T(8,128)} %param.16), kind=kLoop, calls=%fused_computation.17 | loop fusion | flops 4587520 | bytes 18350080 | tf_op jit(solution)/shard_map/concatenate | solution.py:139
  129.9 8.3 %gather_fusion = f32[14,5,32,1024]{3,2,1,0:T(8,128)} fusion(f32[14,5,32,1024]{3,2,1,0:T(8,128)} %pad_maximum_fusion.4, s32[1024]{0:T(1024)} %pad_clamp_fusion.1), kind=kCustom, calls=%fused_computation.2 | custom fusion | bytes 18350136 | tf_op jit(solution)/shard_map/jit(_take)/gather | solution.py:151
  153.6 8.4 %fusion.151 = f32[14,160,32]{2,1,0:T(8,128)} fusion(f32[14,160,1024]{2,1,0:T(8,128)} %fusion.7, s32[32]{0:T(128)S(1)} %copy-done.69), kind=kOutput, calls=%fused_computation.347 | convolution fusion | flops 880836608 | bytes 9461888 | tf_op jit(solution)/shard_map/vmap()/dot_general | solution.py:48
  191.6 7.8 %collective-permute-start.6 = (f32[7,6,5,1024]{3,0,2,1:T(8,128)}, f32[7,6,5,1024]{3,0,2,1:T(8,128)}, u32[]{:S(2)}, u32[]{:S(2)}) collective-permute-start(f32[7,6,5,1024]{3,0,2,1:T(8,128)} %copy.886), channel_id=1, source_target_pairs={{1,0},{2,1},{3,2},{4,3},{5,4},{6,5},{7,6},{8,7},{9,8},{10,9},{11,1... | collective-permute-start | bytes 2580488 | tf_op jit(solution)/shard_map/ppermute | solution.py:19
  235.2 12.2 %copy.1000 = f32[42,6,5,1024]{3,2,1,0:T(8,128)} copy(f32[42,6,5,1024]{3,1,2,0:T(8,128)} %copy_dynamic-update-slice_fusion.4) | data formatting | bytes 10321920 | tf_op jit(solution)/shard_map/reshape | solution.py:204
  253.7 8.0 %pad_maximum_fusion = (f32[14,5,33,1024]{3,2,1,0:T(8,128)S(1)}, f32[14,5,33,1024]{3,2,1,0:T(8,128)S(1)}) fusion(f32[14,5,32,1024]{3,2,1,0:T(8,128)} %copy-done.2, f32[14,5,1,1024]{3,2,1,0:T(1,128)S(1)} %bitcast.664, f32[14,5,1,1024]{3,2,1,0:T(1,128)S(1)} %bitcast.666), kind=kLoop, calls=%fused_computation.3 | loop fusion | flops 4730880 | bytes 28672000 | tf_op jit(solution)/shard_map/vmap()/concatenate | solution.py:75
  288.9 11.4 %bitcast_subtract_fusion.1 = f32[14,5,33,1024]{3,2,0,1:T(8,128)} fusion(f32[5,14,33,1024]{3,2,1,0:T(8,128)} %bitcast_dynamic-update-slice_fusion.2, f32[14,5,33,1024]{3,2,1,0:T(8,128)S(1)} %get-tuple-element.58, f32[14,5,33,1024]{3,2,1,0:T(8,128)S(1)} %get-tuple-element.57), kind=kLoop, calls=%fused_computation.8 | loop fusion | flops 9461760 | bytes 37847040 | tf_op jit(solution)/shard_map/vmap()/sub | solution.py:34
  300.6 11.6 %fusion.215 = (f32[14,5,32,1024]{3,2,1,0:T(8,128)S(1)}, f32[14,5,32,1024]{3,2,1,0:T(8,128)}) fusion(f32[14,5,32,1024]{3,2,1,0:T(8,128)} %copy-done.2, f32[14,5,32,1]{3,2,1,0:T(8,128)S(1)} %slice-done.12, f32[14,5,32,1023]{3,2,1,0:T(8,128)} %slice.836, f32[14,5,32,32]{3,2,1,0:T(8,128)S(1)} %reshape.2108, s32[32]{0:T(128)S(1)} %copy-done.72, ...), kind=kOutput, calls=%fused_computation.486 | convolution fusion | flops 887717888 | bytes 36988032 | tf_op jit(solution)/shard_map/vmap()/dot_general | solution.py:56
  319.9 10.7 %copy_subtract_fusion.2 = f32[14,5,32,1024]{3,2,1,0:T(8,128)S(1)} fusion(f32[14,5,32,1024]{3,2,1,0:T(8,128)} %get-tuple-element.117, f32[14,5,32,1024]{3,2,1,0:T(8,128)} %gather_fusion, pred[14]{0:T(512)(128)(4,1)S(1)} %compare_and_fusion.2, pred[14]{0:T(512)(128)(4,1)S(1)} %iota_compare_fusion.17, f32[5,14,32,1024]{3,2,1,0:T(8,128)} %copy-done.22), kind=kLoop, calls=%fused_computation.42 | loop fusion | flops 13762560 | bytes 36700188 | tf_op jit(solution)/shard_map/vmap()/sub | solution.py:34
  338.9 8.4 %fusion.13 = f32[14,5,32,1024]{3,2,0,1:T(8,128)S(1)} fusion(f32[14,5,32,32]{3,2,0,1:T(8,128)S(1)} %copy-done.16, f32[14,5,32,992]{3,2,0,1:T(8,128)} %copy.1149, f32[14,5,32,32]{3,2,0,1:T(8,128)} %squeeze.111, pred[1024]{0:T(1024)(128)(4,1)S(1)} %copy-done.63, f32[14,5,32,1024]{3,2,1,0:T(8,128)} %gather_fusion, pred[14]{0:T(512)(128)(4,1)S(1)} %compare_and_fusion.2, ...), kind=kLoop, calls=%fused_computation.46 | loop fusion | flops 11468800 | bytes 27812892 | tf_op jit(solution)/shard_map/vmap()/add | solution.py:23
  355.8 10.4 %bitcast_subtract_fusion.4 = f32[14,5,32,1024]{3,2,0,1:T(8,128)} fusion(f32[5,14,32,1024]{3,2,1,0:T(8,128)} %bitcast_dynamic-update-slice_fusion.10, f32[14,5,32,32]{3,2,0,1:T(8,128)S(1)} %copy-done.16, f32[14,5,32,992]{3,2,0,1:T(8,128)} %copy.1149, f32[14,5,32,32]{3,2,0,1:T(8,128)S(1)} %copy-done.23, pred[1024]{0:T(1024)(128)(4,1)S(1)} %copy-done.63, ...), kind=kLoop, calls=%fused_computation.32 | loop fusion | flops 18350080 | bytes 36987932 | tf_op jit(solution)/shard_map/vmap()/sub | solution.py:34
  383.2 23.5 %fusion.11 = f32[14,5,32,1024]{3,2,1,0:T(8,128)S(1)} fusion(f32[14,5,32,1024]{3,2,1,0:T(8,128)} %copy-done.6, f32[14,5,32,1024]{3,2,0,1:T(8,128)} %copy_select_fusion, pred[14]{0:T(512)(128)(4,1)S(1)} %iota_compare_fusion.17, f32[14,5,32,1024]{3,2,1,0:T(8,128)} %gather_fusion, pred[14]{0:T(512)(128)(4,1)S(1)} %compare_and_fusion.2, ...), kind=kLoop, calls=%fused_computation.40 | loop fusion | flops 27525120 | bytes 73974816 | tf_op jit(solution)/shard_map/jit(_where)/select_n | solution.py:207
  479.4 9.5 %copy.1152 = f32[14,5,32,1023]{3,2,0,1:T(8,128)} copy(f32[14,5,32,1023]{3,2,1,0:T(8,128)} %slice.888) | data formatting | bytes 18332160
  500.4 7.9 %copy.1006 = f32[42,6,5,1024]{3,2,1,0:T(8,128)} copy(f32[42,6,5,1024]{3,1,2,0:T(8,128)S(1)} %copy_dynamic-update-slice_fusion) | data formatting | bytes 10321920 | tf_op jit(solution)/shard_map/reshape | solution.py:204
  517.9 8.4 %pad_maximum_fusion.2 = (f32[14,5,33,1024]{3,2,1,0:T(8,128)S(1)}, f32[14,5,33,1024]{3,2,1,0:T(8,128)S(1)}) fusion(f32[14,5,32,1024]{3,2,1,0:T(8,128)} %copy-done, f32[14,5,1,1024]{3,2,1,0:T(1,128)S(1)} %bitcast.665, f32[14,5,1,1024]{3,2,1,0:T(1,128)S(1)} %bitcast.667), kind=kLoop, calls=%fused_computation.5 | loop fusion | flops 4730880 | bytes 28672000 | tf_op jit(solution)/shard_map/vmap()/concatenate | solution.py:75
  553.5 11.3 %bitcast_subtract_fusion = f32[14,5,33,1024]{3,2,0,1:T(8,128)} fusion(f32[5,14,33,1024]{3,2,1,0:T(8,128)} %bitcast_dynamic-update-slice_fusion, f32[14,5,33,1024]{3,2,1,0:T(8,128)S(1)} %get-tuple-element.54, f32[14,5,33,1024]{3,2,1,0:T(8,128)S(1)} %get-tuple-element.53), kind=kLoop, calls=%fused_computation.7 | loop fusion | flops 9461760 | bytes 37847040 | tf_op jit(solution)/shard_map/vmap()/sub | solution.py:34
  571.8 13.3 %select_reduce_fusion.1 = (f32[14,5,16,16]{0,3,2,1:T(8,128)S(1)}, f32[14,5,16,16]{0,3,2,1:T(8,128)S(1)}) fusion(f32[14,5,16,2,16,2]{0,5,4,3,2,1:T(2,128)} %bitcast.651, f32[14,5,16,2,16,2]{0,5,4,3,2,1:T(2,128)} %bitcast.652, pred[14]{0:T(512)(128)(4,1)S(1)} %copy-done.90, f32[14,5,16,2,16,2]{0,5,4,3,2,1:T(2,128)} %bitcast.653, ...), kind=kLoop, calls=%fused_computation.50 | loop fusion | flops 250880 | bytes 1290254 | tf_op jit(solution)/shard_map/reduce_sum | solution.py:213
  591.1 7.9 %collective-permute-start.18 = (f32[14,1280]{1,0:T(8,128)S(1)}, f32[14,1280]{1,0:T(8,128)}, u32[]{:S(2)}, u32[]{:S(2)}) collective-permute-start(f32[14,1280]{1,0:T(8,128)S(1)} %copy.963), channel_id=1, source_target_pairs={{1,0},{2,1},{3,2},{4,3},{5,4},{6,5},{7,6},{8,7},{9,8},{10,9},{11,1... | collective-permute-start | bytes 215048 | tf_op jit(solution)/shard_map/ppermute | solution.py:19
  609.7 11.6 %copy_add_fusion.8 = (f32[14,5,32,1024]{3,2,0,1:T(8,128)S(1)}, f32[14,5,32,1024]{3,2,0,1:T(8,128)}) fusion(f32[14,5,32,1024]{3,2,1,0:T(8,128)} %copy-done, f32[14,5,32,1]{3,2,0,1:T(8,128)S(1)} %copy.1151, f32[14,5,32,1023]{3,2,0,1:T(8,128)} %copy.1152, f32[14,5,32,32]{3,2,0,1:T(8,128)S(1)} %dot_general.71, s32[32]{0:T(128)S(1)} %copy-done.72, ...), kind=kOutput, calls=%fused_computation.472 | convolution fusion | flops 887717888 | bytes 36988032 | tf_op jit(solution)/shard_map/vmap()/dot_general | solution.py:56
  628.6 20.2 %bitcast_subtract_fusion.2 = (f32[14,5,32,1024]{3,2,0,1:T(8,128)}, f32[14,5,32,1024]{3,2,0,1:T(8,128)}) fusion(f32[14,5,32,1024]{3,2,0,1:T(8,128)} %get-tuple-element.119, f32[5,14,32,1024]{3,2,1,0:T(8,128)} %copy-done.21, f32[14,5,32,1024]{3,2,1,0:T(8,128)} %copy-done, f32[14,5,32,32]{3,2,0,1:T(8,128)S(1)} %copy-done.12, f32[14,5,32,992]{3,2,0,1:T(8,128)} %copy.1153, ...), kind=kLoop, calls=%fused_computation.30 | loop fusion | flops 16056320 | bytes 55337984 | tf_op jit(solution)/shard_map/vmap()/sub | solution.py:34
  663.6 10.5 %bitcast_subtract_fusion.3 = f32[14,5,32,1024]{3,2,0,1:T(8,128)} fusion(f32[5,14,32,1024]{3,2,1,0:T(8,128)} %bitcast_dynamic-update-slice_fusion.6, f32[14,5,32,32]{3,2,0,1:T(8,128)S(1)} %copy-done.12, f32[14,5,32,992]{3,2,0,1:T(8,128)} %copy.1153, f32[14,5,32,32]{3,2,0,1:T(8,128)S(1)} %squeeze.122, pred[1024]{0:T(1024)(128)(4,1)S(1)} %copy-done.64, ...), kind=kLoop, calls=%fused_computation.31 | loop fusion | flops 13762560 | bytes 36987904 | tf_op jit(solution)/shard_map/vmap()/sub | solution.py:34
  686.6 25.3 %fusion.2 = f32[14,5,32,1024]{3,2,0,1:T(8,128)} fusion(f32[14,5,33,1024]{3,2,0,1:T(8,128)} %bitcast_subtract_fusion, f32[14,5,32,1024]{3,2,0,1:T(8,128)} %bitcast_subtract_fusion.3, f32[14,5,32,992]{3,2,0,1:T(8,128)} %bitcast.630, f32[14,5,32,32]{3,2,0,1:T(8,128)} %slice.885, f32[14,5,32,1024]{3,2,0,1:T(8,128)} %get-tuple-element.51, ...), kind=kOutput, calls=%fused_computation.14 | convolution fusion | flops 904060928 | bytes 65374336 | tf_op jit(solution)/shard_map/vmap()/dot_general | solution.py:56
  711.9 13.3 %fusion.8 = f32[14,5,32,1024]{3,2,1,0:T(8,128)} fusion(f32[14,5,32,1024]{3,2,1,0:T(8,128)} %copy-done, f32[14,5,32,1024]{3,2,0,1:T(8,128)} %fusion.2, pred[14]{0:T(512)(128)(4,1)S(1)} %copy-done.61), kind=kLoop, calls=%fused_computation.36 | loop fusion | flops 4587520 | bytes 27525134 | tf_op jit(solution)/shard_map/jit(_where)/select_n | solution.py:207
  (566 shorter events, 470.3 us)
Async XLA Ops:
  6.2 66.0 %copy-start.29 = (f32[3,160,32]{2,1,0:T(8,128)}, f32[3,160,32]{2,1,0:T(8,128)S(1)}, u32[]{:S(2)}) copy-start(f32[3,160,32]{2,1,0:T(8,128)S(1)} %copy.828) | copy-start | bytes 184324
  11.8 103.0 %collective-permute-start.1 = (f32[5,1024]{1,0:T(8,128)}, f32[5,1024]{1,0:T(8,128)}, u32[]{:S(2)}, u32[]{:S(2)}) collective-permute-start(f32[5,1024]{1,0:T(8,128)} %slice_bitcast_fusion.30), channel_id=1, source_target_pairs={{1,0},{2,1},{3,2},{4,3},{5,4},{6,5},{7,6},{8,7},{9,8},{10,9},{11,1... | collective-permute-start | bytes 61448 | tf_op jit(solution)/shard_map/ppermute | solution.py:19
  20.8 94.0 %collective-permute-start = (f32[5,1024]{1,0:T(8,128)}, f32[5,1024]{1,0:T(8,128)}, u32[]{:S(2)}, u32[]{:S(2)}) collective-permute-start(f32[5,1024]{1,0:T(8,128)} %slice_bitcast_fusion.31), channel_id=1, source_target_pairs={{0,1},{1,2},{2,3},{3,4},{4,5},{5,6},{6,7},{7,8},{8,9},{9,10},{10,1... | collective-permute-start | bytes 61448 | tf_op jit(solution)/shard_map/ppermute | solution.py:19
  28.5 91.6 %collective-permute-start.3 = (f32[2,5,32,1024]{3,2,1,0:T(8,128)}, f32[2,5,32,1024]{3,2,1,0:T(8,128)}, u32[]{:S(2)}, u32[]{:S(2)}) collective-permute-start(f32[2,5,32,1024]{3,2,1,0:T(8,128)} %get-tuple-element.62), channel_id=1, source_target_pairs={{1,0},{2,1},{3,2},{4,3},{5,4},{6,5},{7,6},{8,7},{9,8},{10,9},{11,1... | collective-permute-start | bytes 3932168 | tf_op jit(solution)/shard_map/ppermute | solution.py:19
  36.4 83.7 %collective-permute-start.2 = (f32[2,5,32,1024]{3,2,1,0:T(8,128)}, f32[2,5,32,1024]{3,2,1,0:T(8,128)}, u32[]{:S(2)}, u32[]{:S(2)}) collective-permute-start(f32[2,5,32,1024]{3,2,1,0:T(8,128)} %get-tuple-element.61), channel_id=1, source_target_pairs={{0,1},{1,2},{2,3},{3,4},{4,5},{5,6},{6,7},{7,8},{8,9},{9,10},{10,1... | collective-permute-start | bytes 3932168 | tf_op jit(solution)/shard_map/ppermute | solution.py:19
  72.2 34.6 %copy-start.36 = (f32[3,5,32,32]{3,2,0,1:T(8,128)}, f32[3,5,32,32]{3,2,0,1:T(8,128)S(1)}, u32[]{:S(2)}) copy-start(f32[3,5,32,32]{3,2,0,1:T(8,128)S(1)} %squeeze_stack_squeeze.12) | copy-start | bytes 184324
  72.3 34.5 %copy-start.56 = (f32[5,3,32,32]{3,2,0,1:T(8,128)}, f32[5,3,32,32]{3,2,0,1:T(8,128)S(1)}, u32[]{:S(2)}) copy-start(f32[5,3,32,32]{3,2,0,1:T(8,128)S(1)} %constant_dynamic-update-slice_fusion.11) | copy-start | bytes 184324
  74.2 308.9 %copy-start.60 = (pred[14]{0:T(512)(128)(4,1)}, pred[14]{0:T(512)(128)(4,1)S(1)}, u32[]{:S(2)}) copy-start(pred[14]{0:T(512)(128)(4,1)S(1)} %iota_compare_fusion.17) | copy-start | bytes 46
  181.9 35.9 %collective-permute-start.4 = (f32[7,6,5,1024]{3,0,2,1:T(8,128)S(1)}, f32[7,6,5,1024]{3,0,2,1:T(8,128)}, u32[]{:S(2)}, u32[]{:S(2)}) collective-permute-start(f32[7,6,5,1024]{3,0,2,1:T(8,128)S(1)} %copy.884), channel_id=1, source_target_pairs={{0,1},{1,2},{2,3},{3,4},{4,5},{5,6},{6,7},{7,8},{8,9},{9,10},{10,1... | collective-permute-start | bytes 2580488 | tf_op jit(solution)/shard_map/ppermute | solution.py:19
  186.0 34.5 %collective-permute-start.5 = (f32[7,6,5,1024]{3,0,2,1:T(8,128)S(1)}, f32[7,6,5,1024]{3,0,2,1:T(8,128)}, u32[]{:S(2)}, u32[]{:S(2)}) collective-permute-start(f32[7,6,5,1024]{3,0,2,1:T(8,128)S(1)} %copy.884), channel_id=1, source_target_pairs={{0,2},{1,3},{2,4},{3,5},{4,6},{5,7},{6,8},{7,9},{8,10},{9,11},{10,... | collective-permute-start | bytes 2580488 | tf_op jit(solution)/shard_map/ppermute | solution.py:19
  191.6 31.6 %collective-permute-start.6 = (f32[7,6,5,1024]{3,0,2,1:T(8,128)}, f32[7,6,5,1024]{3,0,2,1:T(8,128)}, u32[]{:S(2)}, u32[]{:S(2)}) collective-permute-start(f32[7,6,5,1024]{3,0,2,1:T(8,128)} %copy.886), channel_id=1, source_target_pairs={{1,0},{2,1},{3,2},{4,3},{5,4},{6,5},{7,6},{8,7},{9,8},{10,9},{11,1... | collective-permute-start | bytes 2580488 | tf_op jit(solution)/shard_map/ppermute | solution.py:19
  199.5 33.0 %collective-permute-start.7 = (f32[7,6,5,1024]{3,0,2,1:T(8,128)}, f32[7,6,5,1024]{3,0,2,1:T(8,128)}, u32[]{:S(2)}, u32[]{:S(2)}) collective-permute-start(f32[7,6,5,1024]{3,0,2,1:T(8,128)} %copy.886), channel_id=1, source_target_pairs={{2,0},{3,1},{4,2},{5,3},{6,4},{7,5},{8,6},{9,7},{10,8},{11,9},{12,... | collective-permute-start | bytes 2580488 | tf_op jit(solution)/shard_map/ppermute | solution.py:19
  434.9 58.5 %collective-permute-start.12 = (f32[7,6,5,1024]{3,0,2,1:T(8,128)}, f32[7,6,5,1024]{3,0,2,1:T(8,128)}, u32[]{:S(2)}, u32[]{:S(2)}) collective-permute-start(f32[7,6,5,1024]{3,0,2,1:T(8,128)} %copy.940), channel_id=1, source_target_pairs={{0,1},{1,2},{2,3},{3,4},{4,5},{5,6},{6,7},{7,8},{8,9},{9,10},{10,1... | collective-permute-start | bytes 2580488 | tf_op jit(solution)/shard_map/ppermute | solution.py:19
  442.9 52.3 %collective-permute-start.13 = (f32[7,6,5,1024]{3,0,2,1:T(8,128)}, f32[7,6,5,1024]{3,0,2,1:T(8,128)}, u32[]{:S(2)}, u32[]{:S(2)}) collective-permute-start(f32[7,6,5,1024]{3,0,2,1:T(8,128)} %copy.940), channel_id=1, source_target_pairs={{0,2},{1,3},{2,4},{3,5},{4,6},{5,7},{6,8},{7,9},{8,10},{9,11},{10,... | collective-permute-start | bytes 2580488 | tf_op jit(solution)/shard_map/ppermute | solution.py:19
  446.3 50.6 %collective-permute-start.14 = (f32[7,6,5,1024]{3,0,2,1:T(8,128)}, f32[7,6,5,1024]{3,0,2,1:T(8,128)}, u32[]{:S(2)}, u32[]{:S(2)}) collective-permute-start(f32[7,6,5,1024]{3,0,2,1:T(8,128)} %copy.942), channel_id=1, source_target_pairs={{1,0},{2,1},{3,2},{4,3},{5,4},{6,5},{7,6},{8,7},{9,8},{10,9},{11,1... | collective-permute-start | bytes 2580488 | tf_op jit(solution)/shard_map/ppermute | solution.py:19
  454.2 44.5 %collective-permute-start.15 = (f32[7,6,5,1024]{3,0,2,1:T(8,128)}, f32[7,6,5,1024]{3,0,2,1:T(8,128)}, u32[]{:S(2)}, u32[]{:S(2)}) collective-permute-start(f32[7,6,5,1024]{3,0,2,1:T(8,128)} %copy.942), channel_id=1, source_target_pairs={{2,0},{3,1},{4,2},{5,3},{6,4},{7,5},{8,6},{9,7},{10,8},{11,9},{12,... | collective-permute-start | bytes 2580488 | tf_op jit(solution)/shard_map/ppermute | solution.py:19
  587.3 138.0 %collective-permute-start.16 = (f32[14,1280]{1,0:T(8,128)S(1)}, f32[14,1280]{1,0:T(8,128)}, u32[]{:S(2)}, u32[]{:S(2)}) collective-permute-start(f32[14,1280]{1,0:T(8,128)S(1)} %copy.963), channel_id=1, source_target_pairs={{0,1},{1,2},{2,3},{3,4},{4,5},{5,6},{6,7},{7,8},{8,9},{9,10},{10,1... | collective-permute-start | bytes 215048 | tf_op jit(solution)/shard_map/ppermute | solution.py:19
  589.2 138.2 %collective-permute-start.17 = (f32[14,1280]{1,0:T(8,128)S(1)}, f32[14,1280]{1,0:T(8,128)}, u32[]{:S(2)}, u32[]{:S(2)}) collective-permute-start(f32[14,1280]{1,0:T(8,128)S(1)} %copy.963), channel_id=1, source_target_pairs={{0,2},{1,3},{2,4},{3,5},{4,6},{5,7},{6,8},{7,9},{8,10},{9,11},{10,... | collective-permute-start | bytes 215048 | tf_op jit(solution)/shard_map/ppermute | solution.py:19
  591.1 143.9 %collective-permute-start.18 = (f32[14,1280]{1,0:T(8,128)S(1)}, f32[14,1280]{1,0:T(8,128)}, u32[]{:S(2)}, u32[]{:S(2)}) collective-permute-start(f32[14,1280]{1,0:T(8,128)S(1)} %copy.963), channel_id=1, source_target_pairs={{1,0},{2,1},{3,2},{4,3},{5,4},{6,5},{7,6},{8,7},{9,8},{10,9},{11,1... | collective-permute-start | bytes 215048 | tf_op jit(solution)/shard_map/ppermute | solution.py:19
  599.0 139.7 %collective-permute-start.19 = (f32[14,1280]{1,0:T(8,128)S(1)}, f32[14,1280]{1,0:T(8,128)}, u32[]{:S(2)}, u32[]{:S(2)}) collective-permute-start(f32[14,1280]{1,0:T(8,128)S(1)} %copy.963), channel_id=1, source_target_pairs={{2,0},{3,1},{4,2},{5,3},{6,4},{7,5},{8,6},{9,7},{10,8},{11,9},{12,... | collective-permute-start | bytes 215048 | tf_op jit(solution)/shard_map/ppermute | solution.py:19
  605.5 137.5 %collective-permute-start.8 = (f32[14,1280]{1,0:T(8,128)}, f32[14,1280]{1,0:T(8,128)}, u32[]{:S(2)}, u32[]{:S(2)}) collective-permute-start(f32[14,1280]{1,0:T(8,128)} %copy.907), channel_id=1, source_target_pairs={{0,1},{1,2},{2,3},{3,4},{4,5},{5,6},{6,7},{7,8},{8,9},{9,10},{10,1... | collective-permute-start | bytes 215048 | tf_op jit(solution)/shard_map/ppermute | solution.py:19
  725.2 17.9 %collective-permute-start.9 = (f32[14,1280]{1,0:T(8,128)}, f32[14,1280]{1,0:T(8,128)S(1)}, u32[]{:S(2)}, u32[]{:S(2)}) collective-permute-start(f32[14,1280]{1,0:T(8,128)} %copy.907), channel_id=1, source_target_pairs={{0,2},{1,3},{2,4},{3,5},{4,6},{5,7},{6,8},{7,9},{8,10},{9,11},{10,... | collective-permute-start | bytes 215048 | tf_op jit(solution)/shard_map/ppermute | solution.py:19
  727.4 15.7 %collective-permute-start.10 = (f32[14,1280]{1,0:T(8,128)}, f32[14,1280]{1,0:T(8,128)S(1)}, u32[]{:S(2)}, u32[]{:S(2)}) collective-permute-start(f32[14,1280]{1,0:T(8,128)} %copy.907), channel_id=1, source_target_pairs={{1,0},{2,1},{3,2},{4,3},{5,4},{6,5},{7,6},{8,7},{9,8},{10,9},{11,1... | collective-permute-start | bytes 215048 | tf_op jit(solution)/shard_map/ppermute | solution.py:19
  735.1 8.1 %collective-permute-start.11 = (f32[14,1280]{1,0:T(8,128)}, f32[14,1280]{1,0:T(8,128)S(1)}, u32[]{:S(2)}, u32[]{:S(2)}) collective-permute-start(f32[14,1280]{1,0:T(8,128)} %copy.907), channel_id=1, source_target_pairs={{2,0},{3,1},{4,2},{5,3},{6,4},{7,5},{8,6},{9,7},{10,8},{11,9},{12,... | collective-permute-start | bytes 215048 | tf_op jit(solution)/shard_map/ppermute | solution.py:19
  (110 other events, 773.3 us)
where the time goes:
time: 763 us; the launch traced here: 756 us
  other arithmetic  308 us (40%)
  local copies, waits for them, and re-layouts  262 us (34%)
  matrix products  90.1 us (12%)
  starting transfers between devices  81 us (11%)
  between operations  7.84 us (1%)
    sub x11, other arithmetic, face_flux(): return 0.5 * jnp.stack(pieces) - 0.5 * signal[direction] * jump_q  85.8 us
    ppermute x20, starting transfers between devices, shifted(): return lax.ppermute(block, axis, route)  81 us
    dot_general x6, matrix products, spread_lanes(): jnp.dot(layer.reshape(fields * edge_len, other_len), place, precision=lax...  63.8 us
    unnamed x252, local copies, waits for them, and re-layouts  63.5 us
    unnamed x67, other arithmetic  54.5 us
    select_n x2, other arithmetic, fine_substep(): jnp.where(live_slot[:, None, None, None], advanced, 0.0)  36.8 us
    add x12, other arithmetic, face_flux(): total_q = left_q + right_q  29 us
    dot_general x6, matrix products, pick_lanes(): jnp.dot(patch_state.reshape(fields * edge_len, plane_len), place.T, preci...  25.9 us
  transfers between devices with their start and end apart: 20, of which 1 were waited for; matrix products, arithmetic and copies ran while one was open for 36% of the time, Pallas kernels for 0%

commit v1 on v0

v1 whole, which is shorter than its diff:
```python
import functools

import jax
import jax.numpy as jnp
from jax import lax
from jax.experimental import pallas as pl
from jax.experimental.pallas import tpu as pltpu
from jax.sharding import PartitionSpec as P

MESH = pl.DeviceIdType.MESH
OLD, NEW, CAP = 10, 14, 3
PITCH = 48
background = (0.6, -0.4, 0.25)
signal = (1.8, 1.6, 1.45)
sound_sq = 1.44
courant = 0.2
TOP = 31 * 8


def weights(direction):
    up = 0.5 * courant * (signal[direction] - background[direction])
    down = 0.5 * courant * (signal[direction] + background[direction])
    return up, down


X_UP, X_DOWN = weights(0)
Y_UP, Y_DOWN = weights(1)
Z_UP, Z_DOWN = weights(2)
CENTRE = 1.0 - courant * sum(signal)
HALF = 0.5 * courant


def pick(x, idx):
    return jnp.take_along_axis(x, idx, axis=1, mode="promise_in_bounds")


def lane_ids():
    return lax.broadcasted_iota(jnp.int32, (8, 128), 1)


def step(src, s, layer, py, pz, emit):
    lane = lane_ids()
    z = lane % 32
    low, high = lane < 32, lane >= 96
    z0, z31 = z == 0, z == 31
    ghost_idx = lane // 32 + jnp.where(z31, 32, 64)
    for r in range(4):
        rows = pl.ds(8 * r, 8)

        def at(f, j, shift=0):
            return src[s, f, pl.ds(PITCH * j + 8 + 8 * r + shift, 8), :]

        for j in range(8):
            gi = ghost_idx + 4 * j

            def field(f):
                q = at(f, j)
                xm, xp = at(f, j, -1), at(f, j, 1)
                up = at(f, j + 1) if j < 7 else layer[py, f, rows, :]
                dn = at(f, j - 1) if j > 0 else layer[py, f, rows, :]
                g = pick(layer[pz, f, rows, :], gi)
                yp = pltpu.roll(jnp.where(low, up, q), 96, 1)
                ym = pltpu.roll(jnp.where(high, dn, q), 32, 1)
                zp = jnp.where(z31, g, pltpu.roll(q, 127, 1))
                zm = jnp.where(z0, g, pltpu.roll(q, 1, 1))
                lin = (
                    CENTRE * q
                    + X_UP * xp
                    + X_DOWN * xm
                    + Y_UP * yp
                    + Y_DOWN * ym
                    + Z_UP * zp
                    + Z_DOWN * zm
                )
                return lin, (xp, xm, yp, ym, zp, zm)

            lin4, (xp, xm, yp, ym, zp, zm) = field(4)
            dx, dy, dz = xp - xm, yp - ym, zp - zm
            lin, near = field(1)
            emit(r, j, 1, lin - HALF * dx)
            div = near[0] - near[1]
            lin, near = field(2)
            emit(r, j, 2, lin - HALF * dy)
            div = div + (near[2] - near[3])
            lin, near = field(3)
            emit(r, j, 3, lin - HALF * dz)
            div = div + (near[4] - near[5])
            emit(r, j, 4, lin4 - HALF * sound_sq * div)
            lin, near = field(0)
            emit(r, j, 0, lin - HALF * div)


def make_layers(src, s, layer):
    lane = lane_ids()
    slot_of = jnp.where((lane >= 32) & (lane < 96), (lane // 4) % 8, -1)
    pack_idx = 32 * (lane % 4) + jnp.where(lane >= 64, 31, 0)
    for r in range(4):
        for f in range(5):

            def at(j):
                return src[s, f, pl.ds(PITCH * j + 8 + 8 * r, 8), :]

            acc = jnp.where(lane < 64, at(0), at(7))
            for j in range(8):
                acc = jnp.where(slot_of == j, pick(at(j), pack_idx), acc)
            layer[s, f, pl.ds(8 * r, 8), :] = acc


def x_row(src, s, f, x):
    return src[s, f, pl.ds(8 + x, 8, stride=PITCH), :]


def set_x_ghost(dst, s, f, low, high):
    dst[s, f, pl.ds(7, 8, stride=PITCH), :] = low
    dst[s, f, pl.ds(40, 8, stride=PITCH), :] = high


def face_flux(left, right, direction):
    total = [left[f] + right[f] for f in range(5)]
    speed = background[direction]
    normal = total[1 + direction]
    pieces = [speed * total[0] + normal]
    for component in range(3):
        entry = speed * total[1 + component]
        if component == direction:
            entry = entry + total[4]
        pieces.append(entry)
    pieces.append(speed * total[4] + sound_sq * normal)
    return [
        0.5 * pieces[f] - 0.5 * signal[direction] * (right[f] - left[f])
        for f in range(5)
    ]


class Plan:
    def __init__(self, one, two, regs):
        self.one, self.two, self.regs = one, two, regs
        self.windows = [(1, one)] + ([(2, two)] if two else [])
        self.pool = OLD + 2 * sum(w for _, w in self.windows)
        self.reg_windows = [(k + 1, w) for k, w in enumerate(regs) if w]
        self.reg_pool = OLD + 2 * sum(w for _, w in self.reg_windows)
        self.reach = max(2 if two else 1, len(self.reg_windows))


def body_one(plan, n_grp, n_sfc, tab, fine, coarse, mig, cnew, *scr):
    q0, q1, out, c0, c1, cl, l0, l1, inbox, stage, reg, rinbox, rstage, edge, tail, tmp, dsem, ssem, rsem = scr
    devices = n_grp * n_sfc
    me = lax.axis_index("grp") * n_sfc + lax.axis_index("sfc")

    def peer(shift):
        d = lax.rem(me + shift + devices, devices)
        return (d // n_sfc, lax.rem(d, n_sfc))

    shifts = [s for k in range(1, plan.reach + 1) for s in (k, -k)]
    sems = iter(range(64))

    def send(src, dst, shift):
        k = next(sems)
        copy = pltpu.make_async_remote_copy(
            src_ref=src,
            dst_ref=dst,
            send_sem=ssem.at[k],
            recv_sem=rsem.at[k],
            device_id=peer(shift),
            device_id_type=MESH,
        )
        copy.start()
        return copy

    loads = []
    for j in range(8):
        rows, cols = pl.ds(PITCH * j + 8, 32), pl.ds(128 * j, 128)
        loads.append(
            pltpu.make_async_copy(coarse.at[:, :, :, cols], c0.at[:, :, rows, :], dsem.at[j])
        )
    for j in range(8):
        rows, cols = pl.ds(PITCH * j + 8, 32), pl.ds(128 * j, 128)
        loads.append(
            pltpu.make_async_copy(fine.at[:, :, :, cols], q0.at[:, :, rows, :], dsem.at[8 + j])
        )
    for copy in loads:
        copy.start()
    barrier = pltpu.get_barrier_semaphore()
    for shift in shifts:
        pl.semaphore_signal(barrier, inc=1, device_id=peer(shift), device_id_type=MESH)
    pl.semaphore_wait(barrier, len(shifts))
    for copy in loads[:8]:
        copy.wait()
    count, ccount = tab[40], tab[41]
    at_start, at_end = tab[42] == 1, tab[43] == 1

    for f in range(5):
        edge[0, f] = x_row(c0, jnp.maximum(ccount - 1, 0), f, 31)
        edge[1, f] = x_row(c0, 0, f, 0)
    edges = [send(edge.at[0], edge.at[2], 1), send(edge.at[1], edge.at[3], -1)]
    for copy in loads[8:]:
        copy.wait()

    def layers_of(src, layer):
        def one(s, _):
            make_layers(src, s, layer)
            inner_low = tab[30 + s] == 1
            for f in range(5):
                layer[s, f, pl.ds(32, 8), :] = jnp.where(
                    inner_low, x_row(src, s, f, 0), x_row(src, s, f, 31)
                )
            return 0

        lax.fori_loop(0, OLD, one, 0)

    def exchange(layer, part):
        copies = []
        base = 0
        off = 0
        box = inbox.at[part]
        for k, w in plan.windows:
            st = stage.at[part, pl.ds(off, w)]
            for i in range(w):
                src = jnp.maximum(count - w + i, 0)
                for f in range(5):
                    stage[part, off + i, f] = layer[src, f]
            copies.append(send(st, box.at[pl.ds(base, w)], k))
            copies.append(send(layer.at[pl.ds(0, w)], box.at[pl.ds(base + w, w)], -k))
            base += 2 * w
            off += w
        return copies

    def arrive(copies, layer, part):
        for copy in copies:
            copy.wait()

        def one(i, _):
            layer[OLD + i] = inbox[part, i]
            return 0

        lax.fori_loop(0, plan.pool - OLD, one, 0)

    def x_ghosts(src, layer):
        def one(s, _):
            inner_low = tab[30 + s] == 1
            px = tab[s]
            for f in range(5):
                other = layer[px, f, pl.ds(32, 8), :]
                low, high = x_row(src, s, f, 0), x_row(src, s, f, 31)
                set_x_ghost(
                    src,
                    s,
                    f,
                    jnp.where(inner_low, other, low),
                    jnp.where(inner_low, high, other),
                )
            return 0

        lax.fori_loop(0, OLD, one, 0)

    layers_of(q0, l0)
    ghosts = exchange(l0, 0)

    def coarse_layers(s, _):
        make_layers(c0, s, cl)
        return 0

    lax.fori_loop(0, CAP, coarse_layers, 0)
    for copy in edges:
        copy.wait()
    for c in range(CAP):
        last = ccount == c + 1
        for f in range(5):
            low = x_row(c0, c, f, 0)
            high = x_row(c0, c, f, 31)
            if c == 0:
                before = jnp.where(at_start, low, edge[2, f])
            else:
                before = x_row(c0, c - 1, f, 31)
            after = jnp.where(at_end, high, edge[3, f])
            if c < CAP - 1:
                after = jnp.where(last, after, x_row(c0, c + 1, f, 0))
            set_x_ghost(c0, c, f, before, after)

    def coarse_step(s, _):
        def emit(r, j, f, v):
            c1[s, f, pl.ds(32 * j + 8 * r, 8), :] = v

        step(c0, s, cl, s, s, emit)
        return 0

    lax.fori_loop(0, CAP, coarse_step, 0)
    arrive(ghosts, l0, 0)
    x_ghosts(q0, l0)

    def fine_one(s, _):
        def emit(r, j, f, v):
            q1[s, f, pl.ds(PITCH * j + 8 + 8 * r, 8), :] = v

        step(q0, s, l0, tab[10 + s], tab[20 + s], emit)
        return 0

    lax.fori_loop(0, OLD, fine_one, 0)
    layers_of(q1, l1)
    ghosts = exchange(l1, 1)

    lane = lane_ids()
    reg_idx = 64 * ((lane // 32) % 2) + 2 * (lane % 16)
    wide = lax.broadcasted_iota(jnp.int32, (4, 128), 1)

    def register(s, _):
        inner_low = tab[30 + s] == 1
        for f in range(5):
            v = jnp.where(
                inner_low,
                x_row(q0, s, f, 31) + x_row(q1, s, f, 31),
                x_row(q0, s, f, 0) + x_row(q1, s, f, 0),
            )
            v = v + pltpu.roll(v, 127, 1)
            v = v + pltpu.roll(v, 96, 1)
            tmp[f] = pick(v, reg_idx)
            even = tmp[f, pl.ds(0, 4, stride=2), :]
            odd = tmp[f, pl.ds(1, 4, stride=2), :]
            reg[s, pl.ds(4 * f, 4), :] = jnp.where(wide < 64, even, odd)
        reg[s, pl.ds(20, 4), :] = jnp.zeros((4, 128), jnp.float32)
        return 0

    lax.fori_loop(0, OLD, register, 0)
    regs = []
    base, off = 0, 0
    for k, w in plan.reg_windows:
        def fill(i, _):
            src = jnp.maximum(count - w + i, 0)
            rstage[off + i] = reg[src]
            return 0

        lax.fori_loop(0, w, fill, 0)
        regs.append(send(rstage.at[pl.ds(off, w)], rinbox.at[pl.ds(base, w)], k))
        regs.append(send(reg.at[pl.ds(0, w)], rinbox.at[pl.ds(base + w, w)], -k))
        base += 2 * w
        off += w
    arrive(ghosts, l1, 1)
    x_ghosts(q1, l1)

    def fine_two(s, _):
        def emit(r, j, f, v):
            out[s, f, pl.ds(8 * r, 8), pl.ds(128 * j, 128)] = v

        step(q1, s, l1, tab[10 + s], tab[20 + s], emit)
        return 0

    lax.fori_loop(0, 2, fine_two, 0)
    moves = [send(out.at[pl.ds(0, 2)], mig.at[pl.ds(12, 2)], -1)]
    lax.fori_loop(4, OLD, fine_two, 0)

    def fill_tail(f, _):
        for i in range(2):
            for r in range(4):
                tail[i, f, pl.ds(8 * r, 8), :] = out[jnp.maximum(count - 2 + i, 0), f, pl.ds(8 * r, 8), :]
        return 0

    lax.fori_loop(0, 5, fill_tail, 0)
    moves.append(send(tail, mig.at[pl.ds(10, 2)], 1))
    lax.fori_loop(2, 4, fine_two, 0)
    stores = [pltpu.make_async_copy(out, mig.at[pl.ds(0, OLD)], dsem.at[8])]
    stores[0].start()

    for copy in regs:
        copy.wait()

    def take(i, _):
        reg[OLD + i] = rinbox[i]
        return 0

    lax.fori_loop(0, plan.reg_pool - OLD, take, 0)
    right_half = (wide % 32) >= 16
    for c in range(CAP):
        for face in range(2):
            mine = [x_row(c0, c, f, 31 * face) for f in range(5)]
            ghost = [x_row(c0, c, f, 32 if face else -1) for f in range(5)]
            flux = face_flux(mine, ghost, 0) if face else face_flux(ghost, mine, 0)
            for half in range(2):
                k = 44 + c * 8 + face * 4 + half * 2
                has = jnp.where(right_half, tab[k + 1], tab[k]) >= 0
                i0, i1 = jnp.maximum(tab[k], 0), jnp.maximum(tab[k + 1], 0)
                sums = []
                for f in range(5):
                    rows = pl.ds(4 * f, 4)
                    sums.append(0.125 * jnp.where(right_half, reg[i1, rows, :], reg[i0, rows, :]))
                speed = background[0]
                value = [
                    speed * sums[0] + sums[1],
                    speed * sums[1] + sums[4],
                    speed * sums[2],
                    speed * sums[3],
                    speed * sums[4] + sound_sq * sums[1],
                ]
                for f in range(5):
                    tmp[f] = flux[f]
                    part = tmp[f, pl.ds(4 * half, 4), :]
                    rows = pl.ds(128 * half + 31 * face, 4, stride=32)
                    fix = courant * (value[f] - part)
                    fix = -fix if face else fix
                    c1[c, f, rows, :] = c1[c, f, rows, :] + jnp.where(has, fix, 0.0)
    for j in range(8):
        copy = pltpu.make_async_copy(
            c1.at[:, :, pl.ds(32 * j, 32), :], cnew.at[:, :, :, pl.ds(128 * j, 128)], dsem.at[j]
        )
        copy.start()
        stores.append(copy)
    for copy in stores:
        copy.wait()
    for copy in moves:
        copy.wait()


def body_two(tab, mig, cnew, coarse_out, fine_new, held, zeros, in_sem, out_sem):
    jobs = [(c, tab[41] > c, c, cnew, coarse_out) for c in range(CAP)]
    jobs += [(CAP + n, tab[68 + n] >= 0, tab[68 + n], mig, fine_new) for n in range(NEW)]
    for k, live, idx, src, _ in jobs:

        @pl.when(live)
        def _():
            pltpu.make_async_copy(src.at[idx], held.at[k], in_sem.at[k]).start()

    def clear(f, _):
        for r in range(4):
            zeros[f, pl.ds(8 * r, 8), :] = jnp.zeros((8, 1024), jnp.float32)
        return 0

    lax.fori_loop(0, 5, clear, 0)

    def target(k, dst):
        return dst.at[k if k < CAP else k - CAP]

    for k, live, idx, src, dst in jobs:

        @pl.when(jnp.logical_not(live))
        def _():
            pltpu.make_async_copy(zeros, target(k, dst), out_sem.at[k]).start()

    for k, live, idx, src, dst in jobs:

        @pl.when(live)
        def _():
            pltpu.make_async_copy(src.at[idx], held.at[k], in_sem.at[k]).wait()
            pltpu.make_async_copy(held.at[k], target(k, dst), out_sem.at[k]).start()

    for k, live, idx, src, dst in jobs:
        pltpu.make_async_copy(zeros, target(k, dst), out_sem.at[k]).wait()


def tables(plan, coarse_owner, owner_old, owner_new, nbr, reflux):
    me = lax.axis_index(("grp", "sfc"))
    marks = me + jnp.arange(-3, 5, dtype=jnp.int32)

    def starts(owners):
        return jnp.sum((owners[None, :] < marks[:, None]).astype(jnp.int32), axis=1)

    old, new, crs = starts(owner_old), starts(owner_new), starts(coarse_owner)
    total = owner_old.shape[0]
    ids = jnp.arange(total, dtype=jnp.int32)

    def place(p, windows):
        where = p - old[3]
        base = OLD
        for k, w in windows:
            behind = base + w - (old[4 - k] - p)
            ahead = base + w + (p - old[3 + k])
            where = jnp.where(p < old[4 - k], behind, where)
            where = jnp.where(p >= old[3 + k], ahead, where)
            base += 2 * w
        return jnp.clip(where, 0, base - 1)

    slots = jnp.arange(OLD, dtype=jnp.int32)
    mine = (ids[None, :] == old[3] + slots[:, None])[None]
    cols = jnp.stack(
        [
            jnp.maximum(nbr[:, 0], nbr[:, 1]),
            nbr[:, 2],
            nbr[:, 4],
            (nbr[:, 0] >= 0).astype(jnp.int32),
        ]
    )
    got = jnp.sum(jnp.where(mine, cols[:, None, :], 0), axis=2)
    spots = place(got[:3], plan.windows).reshape(-1)
    ccount = crs[4] - crs[3]
    key = jnp.arange(CAP * 8, dtype=jnp.int32)
    wanted = (crs[3] + key // 8) * 8 + key % 8
    code = jnp.where(reflux[:, 0] >= 0, reflux[:, 0] * 8 + reflux[:, 1] * 4 + reflux[:, 2], -1)
    spot = place(ids, plan.reg_windows) + 1
    hit = (code[None, :] == wanted[:, None]) & (key // 8 < ccount)[:, None]
    regs = jnp.sum(jnp.where(hit, spot[None, :], 0), axis=1) - 1
    n = jnp.arange(NEW, dtype=jnp.int32)
    p = new[3] + n
    src = jnp.where(
        p < old[3], OLD + 2 - (old[3] - p), jnp.where(p >= old[4], OLD + 2 + p - old[4], p - old[3])
    )
    src = jnp.where(p < new[4], jnp.clip(src, 0, OLD + 3), -1)
    misc = jnp.stack(
        [
            old[4] - old[3],
            ccount,
            (crs[3] == 0).astype(jnp.int32),
            (crs[4] == coarse_owner.shape[0]).astype(jnp.int32),
        ]
    )
    return jnp.concatenate([spots, got[3], misc, regs, src])


def stage_one(plan, n_grp, n_sfc, tab, fine, coarse):
    f32 = jnp.float32
    big = pl.BlockSpec(memory_space=pl.ANY)
    tall = 8 * PITCH
    wide_stage = plan.pool - OLD
    return pl.pallas_call(
        functools.partial(body_one, plan, n_grp, n_sfc),
        name="advance_level",
        out_shape=(
            jax.ShapeDtypeStruct((OLD + 4, 5, 32, 1024), f32),
            jax.ShapeDtypeStruct((CAP, 5, 32, 1024), f32),
        ),
        in_specs=[pl.BlockSpec(memory_space=pltpu.SMEM), big, big],
        out_specs=(big, big),
        scratch_shapes=[
            pltpu.VMEM((OLD, 5, tall, 128), f32),
            pltpu.VMEM((OLD, 5, tall, 128), f32),
            pltpu.VMEM((OLD, 5, 32, 1024), f32),
            pltpu.VMEM((CAP, 5, tall, 128), f32),
            pltpu.VMEM((CAP, 5, 256, 128), f32),
            pltpu.VMEM((CAP, 5, 32, 128), f32),
            pltpu.VMEM((plan.pool, 5, 40, 128), f32),
            pltpu.VMEM((plan.pool, 5, 40, 128), f32),
            pltpu.VMEM((2, wide_stage, 5, 40, 128), f32),
            pltpu.VMEM((2, wide_stage // 2, 5, 40, 128), f32),
            pltpu.VMEM((plan.reg_pool, 24, 128), f32),
            pltpu.VMEM((plan.reg_pool - OLD, 24, 128), f32),
            pltpu.VMEM(((plan.reg_pool - OLD) // 2, 24, 128), f32),
            pltpu.VMEM((4, 5, 8, 128), f32),
            pltpu.VMEM((2, 5, 32, 1024), f32),
            pltpu.VMEM((5, 8, 128), f32),
            pltpu.SemaphoreType.DMA((16,)),
            pltpu.SemaphoreType.DMA((24,)),
            pltpu.SemaphoreType.DMA((24,)),
        ],
        compiler_params=pltpu.CompilerParams(
            collective_id=0, has_side_effects=True, vmem_limit_bytes=58 * 2**20
        ),
    )(tab, fine, coarse)


def stage_two(tab, mig, cnew):
    f32 = jnp.float32
    big = pl.BlockSpec(memory_space=pl.ANY)
    return pl.pallas_call(
        body_two,
        name="place_patches",
        out_shape=(
            jax.ShapeDtypeStruct((CAP, 5, 32, 1024), f32),
            jax.ShapeDtypeStruct((NEW, 5, 32, 1024), f32),
        ),
        in_specs=[pl.BlockSpec(memory_space=pltpu.SMEM), big, big],
        out_specs=(big, big),
        scratch_shapes=[
            pltpu.VMEM((CAP + NEW, 5, 32, 1024), f32),
            pltpu.VMEM((5, 32, 1024), f32),
            pltpu.SemaphoreType.DMA((CAP + NEW,)),
            pltpu.SemaphoreType.DMA((CAP + NEW,)),
        ],
        compiler_params=pltpu.CompilerParams(vmem_limit_bytes=24 * 2**20),
    )(tab, mig, cnew)


def solution(mesh):
    n_grp, n_sfc = mesh.shape["grp"], mesh.shape["sfc"]
    plan = Plan(7, 1, (10, 10, 10))

    def body(coarse_state, fine_old, coarse_owner, owner_old, owner_new, nbr, reflux):
        tab = tables(plan, coarse_owner, owner_old, owner_new, nbr, reflux)
        mig, cnew = stage_one(plan, n_grp, n_sfc, tab, fine_old, coarse_state)
        return stage_two(tab, mig, cnew)

    split = P(("grp", "sfc"), None, None, None)
    return jax.shard_map(
        body,
        mesh=mesh,
        in_specs=(split, split, P(), P(), P(), P(), P()),
        out_specs=(split, split),
        check_vma=False,
    )
```

time: 763 us -> 119 us (0.16)
  the two profiles are of different devices: /device:TPU:96 before, /device:TPU:0 now
where the time goes in v1:
time: 119 us; the launch traced here: 118 us
  Pallas kernels  91.2 us (77%)
  other arithmetic  15 us (13%)
  local copies, waits for them, and re-layouts  7.38 us (6%)
  between operations  4.63 us (4%)
    pallas_call x1, Pallas kernels, stage_one(): pl.pallas_call(functools.partial(body_one, plan, n_grp, n_sfc), name='adv...  84.3 us
    pallas_call x1, Pallas kernels, stage_two(): pl.pallas_call(body_two, name='place_patches', out_shape=(jax.ShapeDtypeS...  6.93 us
    unnamed x7, local copies, waits for them, and re-layouts  5.24 us
    add x1, other arithmetic, tables(): spot = place(ids, plan.reg_windows) + 1  3.72 us
    select_n x1, other arithmetic, tables(): src = jnp.where(p < new[4], jnp.clip(src, 0, OLD + 3), -1)  2.6 us
    min x1, other arithmetic, place(): return jnp.clip(where, 0, base - 1)  2.49 us

profile of v1, /device:TPU:0, one launch (start us, length us, event | category | flops | bytes accessed | tf_op | source)
XLA Modules:
  0.0 118.2 jit_solution(17695243433537610008)
XLA Ops:
  0.6 0.9 convert_reduce_fusion.2
  1.5 0.9 convert_reduce_fusion
  2.4 0.6 fusion.5
  5.6 0.7 fusion.1
  6.3 0.7 fusion.3
  8.3 2.6 %compare_select_fusion.3 = s32[14]{0:T(128)S(1)} fusion(s32[]{:T(128)} %bitcast.7, s32[]{:T(128)} %bitcast, s32[]{:T(128)} %bitcast.18, s32[]{:T(128)} %bitcast.17), kind=kLoop, calls=%fused_computation.24 | loop fusion | flops 182 | bytes 72 | tf_op jit(solution)/shard_map/jit(_where)/select_n | solution.py:494
  10.9 0.6 iota_add_fusion
  11.5 3.7 %clamp_add_fusion = s32[1024]{0:T(1024)S(1)} fusion(s32[]{:T(128)} %bitcast, s32[]{:T(128)} %bitcast.7, s32[]{:T(128)} %bitcast.6, s32[]{:T(128)} %bitcast.5, s32[]{:T(128)} %bitcast.16, s32[]{:T(128)} %bitcast.15), kind=kLoop, calls=%fused_computation.11 | loop fusion | flops 27648 | bytes 4120 | tf_op jit(solution)/shard_map/add | solution.py:486
  15.2 0.8 compare_select_fusion
  16.1 0.2 select_reduce_fusion.1
  16.3 0.8 fusion
  17.0 0.9 maximum_bitcast_fusion
  18.0 0.1 iota_compare_fusion
  18.1 0.3 select_reduce_fusion
  18.3 0.2 slice_reduce_fusion
  18.5 0.1 copy.12
  18.6 2.5 %select_clamp_fusion = s32[3,10]{1,0:T(4,128)S(1)} fusion(s32[3,10]{1,0:T(4,128)S(1)} %copy.12, s32[]{:T(128)} %bitcast, s32[]{:T(128)} %bitcast.7, s32[]{:T(128)} %bitcast.6, s32[]{:T(128)} %bitcast.5), kind=kLoop, calls=%fused_computation.21 | loop fusion | flops 540 | bytes 256 | tf_op jit(solution)/shard_map/jit(clip)/min | solution.py:468
  21.1 0.1 reshape.174
  21.2 0.6 concatenate.3.tab
  21.8 84.3 %advance_level.1 = (f32[14,5,32,1024]{3,2,1,0:T(8,128)}, f32[3,5,32,1024]{3,2,1,0:T(8,128)}) custom-call(s32[82]{0:T(128)} %concatenate.3.tab, f32[10,5,32,1024]{3,2,1,0:T(8,128)} %fine.1, f32[3,5,32,1024]{3,2,1,0:T(8,128)} %coarse.1), custom_call_target="tpu_custom_call" | custom-call | tf_op jit(solution)/shard_map/advance_level/pallas_call | solution.py:511
  106.1 0.0 copy-done.2
  106.1 3.6 %copy-done = f32[14,5,32,1024]{3,2,1,0:T(8,128)S(1)} copy-done((f32[14,5,32,1024]{3,2,1,0:T(8,128)S(1)}, f32[14,5,32,1024]{3,2,1,0:T(8,128)}, u32[]{:S(2)}) %copy-start) | copy-done | bytes 9175064
  109.7 1.5 %copy-done.1 = f32[3,5,32,1024]{3,2,1,0:T(8,128)S(1)} copy-done((f32[3,5,32,1024]{3,2,1,0:T(8,128)S(1)}, f32[3,5,32,1024]{3,2,1,0:T(8,128)}, u32[]{:S(2)}) %copy-start.1) | copy-done | bytes 1966104
  111.2 6.9 %place_patches.1 = (f32[3,5,32,1024]{3,2,1,0:T(8,128)}, f32[14,5,32,1024]{3,2,1,0:T(8,128)}) custom-call(s32[82]{0:T(128)S(1)} %copy-done.2, f32[14,5,32,1024]{3,2,1,0:T(8,128)S(1)} %copy-done, f32[3,5,32,1024]{3,2,1,0:T(8,128)S(1)} %copy-done.1), custom_call_target="tpu_custom_call" | custom-call | tf_op jit(solution)/shard_map/place_patches/pallas_call | solution.py:550
  (7 shorter events, 0.0 us)
Async XLA Ops:
  21.8 84.3 %copy-start.2 = (s32[82]{0:T(128)S(1)}, s32[82]{0:T(128)}, u32[]{:S(2)}) copy-start(s32[82]{0:T(128)} %concatenate.3.tab) | copy-start | bytes 988
  106.1 3.6 %copy-start = (f32[14,5,32,1024]{3,2,1,0:T(8,128)S(1)}, f32[14,5,32,1024]{3,2,1,0:T(8,128)}, u32[]{:S(2)}) copy-start(f32[14,5,32,1024]{3,2,1,0:T(8,128)} %get-tuple-element.4.mig) | copy-start | bytes 27525124
  109.7 1.5 %copy-start.1 = (f32[3,5,32,1024]{3,2,1,0:T(8,128)S(1)}, f32[3,5,32,1024]{3,2,1,0:T(8,128)}, u32[]{:S(2)}) copy-start(f32[3,5,32,1024]{3,2,1,0:T(8,128)} %get-tuple-element.5.cnew) | copy-start | bytes 5898244

commit v2 on v1

--- a/solution.py
+++ b/solution.py
@@ -135,15 +135,17 @@
 class Plan:
     def __init__(self, one, two, regs):
         self.one, self.two, self.regs = one, two, regs
-        self.windows = [(1, one)] + ([(2, two)] if two else [])
-        self.pool = OLD + 2 * sum(w for _, w in self.windows)
+        self.windows = [(1, one), (2, two)]
+        self.pool = OLD + 2 * (one + two)
         self.reg_windows = [(k + 1, w) for k, w in enumerate(regs) if w]
         self.reg_pool = OLD + 2 * sum(w for _, w in self.reg_windows)
-        self.reach = max(2 if two else 1, len(self.reg_windows))
-
-
-def body_one(plan, n_grp, n_sfc, tab, fine, coarse, mig, cnew, *scr):
-    q0, q1, out, c0, c1, cl, l0, l1, inbox, stage, reg, rinbox, rstage, edge, tail, tmp, dsem, ssem, rsem = scr
+        self.reach = max(2, len(self.reg_windows))
+
+
+def body_one(
+    plan, n_grp, n_sfc, own_old, own_new, own_crs, nbr, flux_map, fine, coarse, mig, cnew, tab2, *scr
+):
+    q0, q1, out, c0, c1, cl, l0, l1, inbox, stage, reg, rinbox, rstage, edge, tail, tmp, tab, dsem, ssem, rsem = scr
     devices = n_grp * n_sfc
     me = lax.axis_index("grp") * n_sfc + lax.axis_index("sfc")
 
@@ -180,6 +182,9 @@
         )
     for copy in loads:
         copy.start()
+    rest_of_tables = fill_tables(
+        plan, me, own_old, own_new, own_crs, nbr, flux_map, tab, tab2
+    )
     barrier = pltpu.get_barrier_semaphore()
     for shift in shifts:
         pl.semaphore_signal(barrier, inc=1, device_id=peer(shift), device_id_type=MESH)
@@ -190,7 +195,7 @@
     at_start, at_end = tab[42] == 1, tab[43] == 1
 
     for f in range(5):
-        edge[0, f] = x_row(c0, jnp.maximum(ccount - 1, 0), f, 31)
+        edge[0, f] = x_row(c0, jnp.clip(ccount - 1, 0, CAP - 1), f, 31)
         edge[1, f] = x_row(c0, 0, f, 0)
     edges = [send(edge.at[0], edge.at[2], 1), send(edge.at[1], edge.at[3], -1)]
     for copy in loads[8:]:
@@ -211,18 +216,24 @@
     def exchange(layer, part):
         copies = []
         base = 0
-        off = 0
         box = inbox.at[part]
+        outer = (lane_ids() < 32) | (lane_ids() >= 96)
         for k, w in plan.windows:
-            st = stage.at[part, pl.ds(off, w)]
-            for i in range(w):
-                src = jnp.maximum(count - w + i, 0)
-                for f in range(5):
-                    stage[part, off + i, f] = layer[src, f]
-            copies.append(send(st, box.at[pl.ds(base, w)], k))
-            copies.append(send(layer.at[pl.ds(0, w)], box.at[pl.ds(base + w, w)], -k))
-            base += 2 * w
-            off += w
+            for side in range(2):
+                st = stage.at[part, pl.ds(base, w)]
+                for i in range(w):
+                    at = TO_PEER + 3 * (base + i)
+                    ix, iy, iz = tab[at], tab[at + 1], tab[at + 2]
+                    for f in range(5):
+                        for r in range(4):
+                            rows = pl.ds(8 * r, 8)
+                            stage[part, base + i, f, rows, :] = jnp.where(
+                                outer, layer[iy, f, rows, :], layer[iz, f, rows, :]
+                            )
+                        rows = pl.ds(32, 8)
+                        stage[part, base + i, f, rows, :] = layer[ix, f, rows, :]
+                copies.append(send(st, box.at[pl.ds(base, w)], -k if side else k))
+                base += w
         return copies
 
     def arrive(copies, layer, part):
@@ -255,6 +266,87 @@
 
     layers_of(q0, l0)
     ghosts = exchange(l0, 0)
+
+    rest_of_tables()
+    arrive(ghosts, l0, 0)
+    x_ghosts(q0, l0)
+
+    def fine_one(s, _):
+        def emit(r, j, f, v):
+            q1[s, f, pl.ds(PITCH * j + 8 + 8 * r, 8), :] = v
+
+        step(q0, s, l0, tab[10 + s], tab[20 + s], emit)
+        return 0
+
+    lax.fori_loop(0, OLD, fine_one, 0)
+    layers_of(q1, l1)
+    ghosts = exchange(l1, 1)
+
+    lane = lane_ids()
+    reg_idx = 64 * ((lane // 32) % 2) + 2 * (lane % 16)
+    wide = lax.broadcasted_iota(jnp.int32, (4, 128), 1)
+
+    def register(s, _):
+        inner_low = tab[30 + s] == 1
+        for f in range(5):
+            v = jnp.where(
+                inner_low,
+                x_row(q0, s, f, 31) + x_row(q1, s, f, 31),
+                x_row(q0, s, f, 0) + x_row(q1, s, f, 0),
+            )
+            v = v + pltpu.roll(v, 127, 1)
+            v = v + pltpu.roll(v, 96, 1)
+            tmp[f] = pick(v, reg_idx)
+            even = tmp[f, pl.ds(0, 4, stride=2), :]
+            odd = tmp[f, pl.ds(1, 4, stride=2), :]
+            reg[s, pl.ds(4 * f, 4), :] = jnp.where(wide < 64, even, odd)
+        reg[s, pl.ds(20, 4), :] = jnp.zeros((4, 128), jnp.float32)
+        return 0
+
+    lax.fori_loop(0, OLD, register, 0)
+    regs = []
+    base, off = 0, 0
+    for k, w in plan.reg_windows:
+        def fill(i, _):
+            src = jnp.clip(count - w + i, 0, OLD - 1)
+            rstage[off + i] = reg[src]
+            return 0
+
+        lax.fori_loop(0, w, fill, 0)
+        regs.append(send(rstage.at[pl.ds(off, w)], rinbox.at[pl.ds(base, w)], k))
+        regs.append(send(reg.at[pl.ds(0, w)], rinbox.at[pl.ds(base + w, w)], -k))
+        base += 2 * w
+        off += w
+    arrive(ghosts, l1, 1)
+    x_ghosts(q1, l1)
+
+    def fine_two(s, _):
+        def emit(r, j, f, v):
+            out[s, f, pl.ds(8 * r, 8), pl.ds(128 * j, 128)] = v
+
+        step(q1, s, l1, tab[10 + s], tab[20 + s], emit)
+        return 0
+
+    lax.fori_loop(0, 2, fine_two, 0)
+    moves = [send(out.at[pl.ds(0, 2)], mig.at[pl.ds(12, 2)], -1)]
+
+    def tail_two(i, _):
+        s = jnp.clip(count - 2 + i, 0, OLD - 1)
+
+        def emit(r, j, f, v):
+            tail[i, f, pl.ds(8 * r, 8), pl.ds(128 * j, 128)] = v
+
+        step(q1, s, l1, tab[10 + s], tab[20 + s], emit)
+        return 0
+
+    lax.fori_loop(0, 2, tail_two, 0)
+    moves.append(send(tail, mig.at[pl.ds(10, 2)], 1))
+    lax.fori_loop(2, 6, fine_two, 0)
+    stores = [pltpu.make_async_copy(out.at[pl.ds(0, 6)], mig.at[pl.ds(0, 6)], dsem.at[8])]
+    stores[0].start()
+    lax.fori_loop(6, OLD, fine_two, 0)
+    stores.append(pltpu.make_async_copy(out.at[pl.ds(6, 4)], mig.at[pl.ds(6, 4)], dsem.at[9]))
+    stores[1].start()
 
     def coarse_layers(s, _):
         make_layers(c0, s, cl)
@@ -285,81 +377,6 @@
         return 0
 
     lax.fori_loop(0, CAP, coarse_step, 0)
-    arrive(ghosts, l0, 0)
-    x_ghosts(q0, l0)
-
-    def fine_one(s, _):
-        def emit(r, j, f, v):
-            q1[s, f, pl.ds(PITCH * j + 8 + 8 * r, 8), :] = v
-
-        step(q0, s, l0, tab[10 + s], tab[20 + s], emit)
-        return 0
-
-    lax.fori_loop(0, OLD, fine_one, 0)
-    layers_of(q1, l1)
-    ghosts = exchange(l1, 1)
-
-    lane = lane_ids()
-    reg_idx = 64 * ((lane // 32) % 2) + 2 * (lane % 16)
-    wide = lax.broadcasted_iota(jnp.int32, (4, 128), 1)
-
-    def register(s, _):
-        inner_low = tab[30 + s] == 1
-        for f in range(5):
-            v = jnp.where(
-                inner_low,
-                x_row(q0, s, f, 31) + x_row(q1, s, f, 31),
-                x_row(q0, s, f, 0) + x_row(q1, s, f, 0),
-            )
-            v = v + pltpu.roll(v, 127, 1)
-            v = v + pltpu.roll(v, 96, 1)
-            tmp[f] = pick(v, reg_idx)
-            even = tmp[f, pl.ds(0, 4, stride=2), :]
-            odd = tmp[f, pl.ds(1, 4, stride=2), :]
-            reg[s, pl.ds(4 * f, 4), :] = jnp.where(wide < 64, even, odd)
-        reg[s, pl.ds(20, 4), :] = jnp.zeros((4, 128), jnp.float32)
-        return 0
-
-    lax.fori_loop(0, OLD, register, 0)
-    regs = []
-    base, off = 0, 0
-    for k, w in plan.reg_windows:
-        def fill(i, _):
-            src = jnp.maximum(count - w + i, 0)
-            rstage[off + i] = reg[src]
-            return 0
-
-        lax.fori_loop(0, w, fill, 0)
-        regs.append(send(rstage.at[pl.ds(off, w)], rinbox.at[pl.ds(base, w)], k))
-        regs.append(send(reg.at[pl.ds(0, w)], rinbox.at[pl.ds(base + w, w)], -k))
-        base += 2 * w
-        off += w
-    arrive(ghosts, l1, 1)
-    x_ghosts(q1, l1)
-
-    def fine_two(s, _):
-        def emit(r, j, f, v):
-            out[s, f, pl.ds(8 * r, 8), pl.ds(128 * j, 128)] = v
-
-        step(q1, s, l1, tab[10 + s], tab[20 + s], emit)
-        return 0
-
-    lax.fori_loop(0, 2, fine_two, 0)
-    moves = [send(out.at[pl.ds(0, 2)], mig.at[pl.ds(12, 2)], -1)]
-    lax.fori_loop(4, OLD, fine_two, 0)
-
-    def fill_tail(f, _):
-        for i in range(2):
-            for r in range(4):
-                tail[i, f, pl.ds(8 * r, 8), :] = out[jnp.maximum(count - 2 + i, 0), f, pl.ds(8 * r, 8), :]
-        return 0
-
-    lax.fori_loop(0, 5, fill_tail, 0)
-    moves.append(send(tail, mig.at[pl.ds(10, 2)], 1))
-    lax.fori_loop(2, 4, fine_two, 0)
-    stores = [pltpu.make_async_copy(out, mig.at[pl.ds(0, OLD)], dsem.at[8])]
-    stores[0].start()
-
     for copy in regs:
         copy.wait()
 
@@ -410,8 +427,8 @@
 
 
 def body_two(tab, mig, cnew, coarse_out, fine_new, held, zeros, in_sem, out_sem):
-    jobs = [(c, tab[41] > c, c, cnew, coarse_out) for c in range(CAP)]
-    jobs += [(CAP + n, tab[68 + n] >= 0, tab[68 + n], mig, fine_new) for n in range(NEW)]
+    jobs = [(c, tab[NEW] > c, c, cnew, coarse_out) for c in range(CAP)]
+    jobs += [(CAP + n, tab[n] >= 0, tab[n], mig, fine_new) for n in range(NEW)]
     for k, live, idx, src, _ in jobs:
 
         @pl.when(live)
@@ -445,67 +462,148 @@
         pltpu.make_async_copy(zeros, target(k, dst), out_sem.at[k]).wait()
 
 
-def tables(plan, coarse_owner, owner_old, owner_new, nbr, reflux):
-    me = lax.axis_index(("grp", "sfc"))
-    marks = me + jnp.arange(-3, 5, dtype=jnp.int32)
-
-    def starts(owners):
-        return jnp.sum((owners[None, :] < marks[:, None]).astype(jnp.int32), axis=1)
-
-    old, new, crs = starts(owner_old), starts(owner_new), starts(coarse_owner)
+TO_PEER = 72
+
+
+def fill_tables(plan, me, own_old, own_new, own_crs, nbr, flux_map, tab, tab2):
+    def start(owners, mark):
+        return jnp.sum((owners[...] < mark).astype(jnp.int32))
+
+    old = [start(own_old, me + k) for k in range(-3, 5)]
+    new = [start(own_new, me + k) for k in range(2)]
+    crs = [start(own_crs, me + k) for k in range(2)]
+    total = own_old.shape[0] * own_old.shape[1]
+    base, end = old[3], old[4]
+    cut, cut_end = base % 8, end % 8
+    prev1, next1 = OLD, OLD + plan.one
+    prev2, next2 = OLD + 2 * plan.one, OLD + 2 * plan.one + plan.two
+
+    def patch(p):
+        p = jnp.clip(p, 0, total - 1)
+        return jnp.maximum(nbr[0, p], nbr[1, p]), nbr[2, p], nbr[4, p]
+
+    def spot(p, u):
+        where = u - base
+        before = prev1 + jnp.where(cut <= 4, u - (base - cut), p - base)
+        after = next1 + jnp.where(cut_end <= 4, p - (end - cut_end), u - end)
+        where = jnp.where(u < base, before, where)
+        where = jnp.where(u < old[2], prev2, where)
+        where = jnp.where(u >= end, after, where)
+        where = jnp.where(u >= old[5], next2, where)
+        return jnp.clip(where, 0, plan.pool - 1)
+
+    def one_patch(s, _):
+        p = base + s
+        nx, ny, nz = patch(p)
+        tab[s] = spot(p, nx)
+        tab[10 + s] = spot(p, ny)
+        tab[20 + s] = spot(p, nz)
+        return 0
+
+    def one_side(s, _):
+        p = base + s
+        tab[30 + s] = (nbr[0, jnp.clip(p, 0, total - 1)] >= 0).astype(jnp.int32)
+        return 0
+
+    lax.fori_loop(0, OLD, one_side, 0)
+    tab[40] = end - base
+    tab[41] = crs[1] - crs[0]
+    tab[42] = (crs[0] == 0).astype(jnp.int32)
+    tab[43] = (crs[1] == 2 * own_crs.shape[1]).astype(jnp.int32)
+
+    def local(u):
+        return jnp.clip(u - base, 0, OLD - 1)
+
+    def to_peers(i, _):
+        own = local(end - cut_end + i)
+        parts = patch(end + i)
+        for k in range(3):
+            tab[TO_PEER + 3 * i + k] = jnp.where(cut_end <= 4, own, local(parts[k]))
+        parts = patch(base - cut + i)
+        for k in range(3):
+            at = TO_PEER + 3 * (plan.one + i) + k
+            tab[at] = jnp.where(cut <= 4, local(parts[k]), local(base + i))
+        return 0
+
+    lax.fori_loop(0, plan.one, to_peers, 0)
+    for i in range(plan.two):
+        for k in range(3):
+            at = TO_PEER + 3 * (2 * plan.one + i) + k
+            tab[at] = local(end - plan.two + i)
+            tab[at + 3 * plan.two] = local(base + i)
+
+    def reg_spot(p):
+        where = p - base
+        at = OLD
+        for k, w in plan.reg_windows:
+            where = jnp.where(p < old[4 - k], at + w - (old[4 - k] - p), where)
+            where = jnp.where(p >= old[3 + k], at + w + (p - old[3 + k]), where)
+            at += 2 * w
+        return jnp.clip(where, 0, at - 1)
+
+    def one_face(e, _):
+        c, face = e // 2, e % 2
+        g = crs[0] + c
+        block = (g + 1) // 2 - 1 + face
+        live = g < crs[1]
+        found = [jnp.int32(-1)] * 4
+        for i in range(8):
+            p = jnp.clip(8 * block + i, 0, total - 1)
+            hit = live & (flux_map[0, p] == g) & (flux_map[1, p] == face)
+            place = reg_spot(p)
+            quarter = flux_map[2, p]
+            for q in range(4):
+                found[q] = jnp.where(hit & (quarter == q), place, found[q])
+        for q in range(4):
+            tab[44 + 4 * e + q] = found[q]
+        return 0
+
+    def one_row(n, _):
+        p = new[0] + n
+        src = p - base
+        src = jnp.where(p < base, OLD + 2 - (base - p), src)
+        src = jnp.where(p >= end, OLD + 2 + (p - end), src)
+        tab2[n] = jnp.where(p < new[1], jnp.clip(src, 0, OLD + 3), -1)
+        return 0
+
+    def rest():
+        lax.fori_loop(0, OLD, one_patch, 0)
+        lax.fori_loop(0, 2 * CAP, one_face, 0)
+        lax.fori_loop(0, NEW, one_row, 0)
+        tab2[NEW] = crs[1] - crs[0]
+
+    return rest
+
+
+def few_cuts(coarse_owner, owner_old, reflux):
     total = owner_old.shape[0]
     ids = jnp.arange(total, dtype=jnp.int32)
 
-    def place(p, windows):
-        where = p - old[3]
-        base = OLD
-        for k, w in windows:
-            behind = base + w - (old[4 - k] - p)
-            ahead = base + w + (p - old[3 + k])
-            where = jnp.where(p < old[4 - k], behind, where)
-            where = jnp.where(p >= old[3 + k], ahead, where)
-            base += 2 * w
-        return jnp.clip(where, 0, base - 1)
-
-    slots = jnp.arange(OLD, dtype=jnp.int32)
-    mine = (ids[None, :] == old[3] + slots[:, None])[None]
-    cols = jnp.stack(
-        [
-            jnp.maximum(nbr[:, 0], nbr[:, 1]),
-            nbr[:, 2],
-            nbr[:, 4],
-            (nbr[:, 0] >= 0).astype(jnp.int32),
-        ]
+    def near(k):
+        edge = owner_old[0] - 1 if k < 0 else owner_old[-1] + 1
+        fill = jnp.full((1,), edge, jnp.int32)
+        if k < 0:
+            return jnp.concatenate([fill, owner_old[:-1]])
+        return jnp.concatenate([owner_old[1:], fill])
+
+    first, last = near(-1) != owner_old, near(1) != owner_old
+    cut = ids % 8
+    wide = first & (cut >= 2) & (cut <= 6)
+    target = reflux[:, 0]
+    coarse_ids = jnp.arange(coarse_owner.shape[0], dtype=jnp.int32)
+    onto = jnp.sum(
+        jnp.where(coarse_ids[:, None] == target[None, :], coarse_owner[:, None], 0), axis=0
     )
-    got = jnp.sum(jnp.where(mine, cols[:, None, :], 0), axis=2)
-    spots = place(got[:3], plan.windows).reshape(-1)
-    ccount = crs[4] - crs[3]
-    key = jnp.arange(CAP * 8, dtype=jnp.int32)
-    wanted = (crs[3] + key // 8) * 8 + key % 8
-    code = jnp.where(reflux[:, 0] >= 0, reflux[:, 0] * 8 + reflux[:, 1] * 4 + reflux[:, 2], -1)
-    spot = place(ids, plan.reg_windows) + 1
-    hit = (code[None, :] == wanted[:, None]) & (key // 8 < ccount)[:, None]
-    regs = jnp.sum(jnp.where(hit, spot[None, :], 0), axis=1) - 1
-    n = jnp.arange(NEW, dtype=jnp.int32)
-    p = new[3] + n
-    src = jnp.where(
-        p < old[3], OLD + 2 - (old[3] - p), jnp.where(p >= old[4], OLD + 2 + p - old[4], p - old[3])
-    )
-    src = jnp.where(p < new[4], jnp.clip(src, 0, OLD + 3), -1)
-    misc = jnp.stack(
-        [
-            old[4] - old[3],
-            ccount,
-            (crs[3] == 0).astype(jnp.int32),
-            (crs[4] == coarse_owner.shape[0]).astype(jnp.int32),
-        ]
-    )
-    return jnp.concatenate([spots, got[3], misc, regs, src])
-
-
-def stage_one(plan, n_grp, n_sfc, tab, fine, coarse):
+    away = jnp.where(target >= 0, onto - owner_old, 0)
+    far = (jnp.abs(away) > 2) | ((away == 2) & ~last) | ((away == -2) & ~first)
+    return ~jnp.any(wide | far)
+
+
+def stage_one(plan, number, n_grp, n_sfc, owners, nbr, flux_map, fine, coarse):
     f32 = jnp.float32
     big = pl.BlockSpec(memory_space=pl.ANY)
+    smem = pl.BlockSpec(memory_space=pltpu.SMEM)
+    vmem = pl.BlockSpec(memory_space=pltpu.VMEM)
     tall = 8 * PITCH
     wide_stage = plan.pool - OLD
     return pl.pallas_call(
@@ -514,9 +612,10 @@
         out_shape=(
             jax.ShapeDtypeStruct((OLD + 4, 5, 32, 1024), f32),
             jax.ShapeDtypeStruct((CAP, 5, 32, 1024), f32),
+            jax.ShapeDtypeStruct((16,), jnp.int32),
         ),
-        in_specs=[pl.BlockSpec(memory_space=pltpu.SMEM), big, big],
-        out_specs=(big, big),
+        in_specs=[vmem] * 3 + [smem] * 2 + [big, big],
+        out_specs=(big, big, smem),
         scratch_shapes=[
             pltpu.VMEM((OLD, 5, tall, 128), f32),
             pltpu.VMEM((OLD, 5, tall, 128), f32),
@@ -527,21 +626,22 @@
             pltpu.VMEM((plan.pool, 5, 40, 128), f32),
             pltpu.VMEM((plan.pool, 5, 40, 128), f32),
             pltpu.VMEM((2, wide_stage, 5, 40, 128), f32),
-            pltpu.VMEM((2, wide_stage // 2, 5, 40, 128), f32),
+            pltpu.VMEM((2, wide_stage, 5, 40, 128), f32),
             pltpu.VMEM((plan.reg_pool, 24, 128), f32),
             pltpu.VMEM((plan.reg_pool - OLD, 24, 128), f32),
             pltpu.VMEM(((plan.reg_pool - OLD) // 2, 24, 128), f32),
             pltpu.VMEM((4, 5, 8, 128), f32),
             pltpu.VMEM((2, 5, 32, 1024), f32),
             pltpu.VMEM((5, 8, 128), f32),
+            pltpu.SMEM((128,), jnp.int32),
             pltpu.SemaphoreType.DMA((16,)),
             pltpu.SemaphoreType.DMA((24,)),
             pltpu.SemaphoreType.DMA((24,)),
         ],
         compiler_params=pltpu.CompilerParams(
-            collective_id=0, has_side_effects=True, vmem_limit_bytes=58 * 2**20
+            collective_id=number, has_side_effects=True, vmem_limit_bytes=58 * 2**20
         ),
-    )(tab, fine, coarse)
+    )(*owners, nbr, flux_map, fine, coarse)
 
 
 def stage_two(tab, mig, cnew):
@@ -562,17 +662,23 @@
             pltpu.SemaphoreType.DMA((CAP + NEW,)),
             pltpu.SemaphoreType.DMA((CAP + NEW,)),
         ],
-        compiler_params=pltpu.CompilerParams(vmem_limit_bytes=24 * 2**20),
+        compiler_params=pltpu.CompilerParams(vmem_limit_bytes=58 * 2**20),
     )(tab, mig, cnew)
 
 
 def solution(mesh):
     n_grp, n_sfc = mesh.shape["grp"], mesh.shape["sfc"]
-    plan = Plan(7, 1, (10, 10, 10))
+    common, general = Plan(1, 1, (10, 1)), Plan(4, 1, (10, 10, 10))
 
     def body(coarse_state, fine_old, coarse_owner, owner_old, owner_new, nbr, reflux):
-        tab = tables(plan, coarse_owner, owner_old, owner_new, nbr, reflux)
-        mig, cnew = stage_one(plan, n_grp, n_sfc, tab, fine_old, coarse_state)
+        owners = (owner_old.reshape(8, -1), owner_new.reshape(8, -1), coarse_owner.reshape(2, -1))
+        args = (owners, nbr.T, reflux.T, fine_old, coarse_state)
+        mig, cnew, tab = lax.cond(
+            few_cuts(coarse_owner, owner_old, reflux),
+            functools.partial(stage_one, common, 0, n_grp, n_sfc),
+            functools.partial(stage_one, general, 1, n_grp, n_sfc),
+            *args,
+        )
         return stage_two(tab, mig, cnew)
 
     split = P(("grp", "sfc"), None, None, None)

time: 119 us -> 81.2 us (0.68)
  Pallas kernels: 91.2 us -> 72.6 us
  other arithmetic: 15 us -> 2.3 us
  local copies, waits for them, and re-layouts: 7.38 us -> 2.9 us
  between operations: 4.63 us -> 2.76 us
    pallas_call x1, Pallas kernels: 84.3 us -> 64.5 us  [stage_one(): pl.pallas_call(functools.partial(body_one, plan, n_grp, n_sfc), name='adv...]
    unnamed x7 -> x0, local copies, waits for them, and re-layouts: 5.24 us -> none
    add x4 -> x0, other arithmetic: 4.98 us -> none  [the longest x1 3.72 us: tables(): spot = place(ids, plan.reg_windows) + 1]
    select_n x2 -> x0, other arithmetic: 3.44 us -> none  [the longest x1 2.6 us: tables(): src = jnp.where(p < new[4], jnp.clip(src, 0, OLD + 3), -1)]
    min x1 -> x0, other arithmetic: 2.49 us -> none  [place(): return jnp.clip(where, 0, base - 1)]
    slice x3, local copies, waits for them, and re-layouts: 1.46 us -> 2.9 us  [the longest x1 1.34 us: near(): edge = owner_old[0] - 1 if k < 0 else owner_old[-1] + 1]
    reduce_or x0 -> x1, other arithmetic: none -> 1.4 us  [few_cuts(): return ~jnp.any(wide | far)]
    reduce_sum x4 -> x1, other arithmetic: 2.24 us -> 0.89 us  [few_cuts(): jnp.sum(jnp.where(coarse_ids[:, None] == target[None, :], coarse_owner[:,...]
where the time goes in v2:
time: 81.2 us; the launch traced here: 80.7 us
  Pallas kernels  72.6 us (89%)
  local copies, waits for them, and re-layouts  2.9 us (4%)
  between operations  2.76 us (3%)
  other arithmetic  2.3 us (3%)
    pallas_call x1, Pallas kernels, stage_one(): pl.pallas_call(functools.partial(body_one, plan, n_grp, n_sfc), name='adv...  64.5 us
    pallas_call x1, Pallas kernels, stage_two(): pl.pallas_call(body_two, name='place_patches', out_shape=(jax.ShapeDtypeS...  8.1 us

profile of v2, /device:TPU:0, one launch (start us, length us, event | category | flops | bytes accessed | tf_op | source)
XLA Modules:
  0.0 80.7 jit_solution(16647108542216786581)
XLA Ops:
  0.6 1.3 %fusion.13 = (s32[1]{0:T(128)}, s32[1]{0:T(128)}) fusion(s32[1024]{0:T(1024)} %param.12), kind=kLoop, calls=%fused_computation.21 | loop fusion | bytes 16 | tf_op jit(solution)/shard_map/slice | solution.py:583
  3.3 0.7 slice.17
  4.0 0.9 %select_reduce_fusion = s32[1024]{0:T(1024)S(1)} fusion(s32[256]{0:T(256)} %param.11, s32[1024]{0:T(1024)S(1)} %bitcast.12), kind=kLoop, calls=%fused_computation | loop fusion | flops 785408 | bytes 9216 | tf_op jit(solution)/shard_map/reduce_sum | solution.py:594
  4.9 0.8 %fusion.14 = (s32[1023]{0:T(1024)S(1)}, s32[1023]{0:T(1024)S(1)}) fusion(s32[1024]{0:T(1024)} %param.12), kind=kLoop, calls=%fused_computation.22 | loop fusion | bytes 16368 | tf_op jit(solution)/shard_map/slice | solution.py:586
  5.7 1.4 %fusion.12 = pred[]{:T(512)} fusion(s32[1024]{0:T(1024)} %param.12, s32[1]{0:T(128)S(6)} %add.15, s32[1023]{0:T(1024)S(1)} %get-tuple-element.53, s32[1024]{0:T(1024)S(1)} %select_reduce_fusion, s32[1024]{0:T(1024)S(1)} %bitcast.13, s32[1023]{0:T(1024)S(1)} %get-tuple-element.52, s32[1]{0:T(128)S(6)} %sub.6), kind=kLoop, calls=%fused_computation.20 | loop fusion | flops 29695 | bytes 20481 | tf_op jit(solution)/shard_map/reduce_or | solution.py:599
  7.8 64.7 %conditional.1 = ((f32[14,5,32,1024]{3,2,1,0:T(8,128)}, f32[3,5,32,1024]{3,2,1,0:T(8,128)S(1)}, s32[16]{0:T(128)S(1)})) conditional(s32[]{:T(128)} %convert_element_type.3, (s32[8,128]{1,0:T(8,128)}, s32[8,128]{1,0:T(8,128)}, s32[2,128]{1,0:T(2,128)}, s32[6,1024]{1,0:T(8,128)}, s32[3,1024]{1,0:T(4,128)}, /*index=5*/f32[10,5,32,1024]{3,2,1,0:T(8,128)}, ...), branch_computations={%region_2.3_spmd, %region_3.4_spmd} | conditional | bytes 8 | solution.py:676
  8.0 64.5 %advance_level.3 = (f32[14,5,32,1024]{3,2,1,0:T(8,128)}, f32[3,5,32,1024]{3,2,1,0:T(8,128)S(1)}, s32[16]{0:T(128)S(1)}) custom-call(s32[8,128]{1,0:T(8,128)} %get-tuple-element.35.own_old, s32[8,128]{1,0:T(8,128)} %get-tuple-element.36.own_new, s32[2,128]{1,0:T(2,128)} %get-tuple-element.37.own_crs, s32[6,1024]{1,0:T(8,128)} %get-tuple-element.38.nbr, ...), custom_call_target="tpu_custom_call" | custom-call | tf_op jit(solution)/shard_map/cond/branch_1_fun/advance_level/pallas_call | solution.py:609
  72.5 8.1 %place_patches.1 = (f32[3,5,32,1024]{3,2,1,0:T(8,128)}, f32[14,5,32,1024]{3,2,1,0:T(8,128)}) custom-call(s32[16]{0:T(128)S(1)} %get-tuple-element.47.tab, f32[14,5,32,1024]{3,2,1,0:T(8,128)} %get-tuple-element.48.mig, f32[3,5,32,1024]{3,2,1,0:T(8,128)S(1)} %get-tuple-element.49.cnew), custom_call_target="tpu_custom_call" | custom-call | tf_op jit(solution)/shard_map/place_patches/pallas_call | solution.py:650

commit v3 on v2

--- a/solution.py
+++ b/solution.py
@@ -38,31 +38,50 @@
     return lax.broadcasted_iota(jnp.int32, (8, 128), 1)
 
 
-def step(src, s, layer, py, pz, emit):
+def halves(q):
+    head = q.astype(jnp.bfloat16)
+    rest = (q - head.astype(jnp.float32)).astype(jnp.bfloat16)
+    return jnp.concatenate([head, rest], axis=1)
+
+
+def set_z_shift(mat):
+    row = lax.broadcasted_iota(jnp.int32, (256, 256), 0) % 128
+    col = lax.broadcasted_iota(jnp.int32, (256, 256), 1)
+    at = col % 128
+    up = (row == at + 1) & (at % 32 != 31) & (col < 128)
+    down = (row == at - 1) & (at % 32 != 0) & (col >= 128)
+    mat[...] = jnp.where(up | down, 1.0, 0.0).astype(jnp.bfloat16)
+
+
+def step(src, s, layer, py, pz, mat, emit):
     lane = lane_ids()
     z = lane % 32
     low, high = lane < 32, lane >= 96
     z0, z31 = z == 0, z == 31
     ghost_idx = lane // 32 + jnp.where(z31, 32, 64)
-    for r in range(4):
-        rows = pl.ds(8 * r, 8)
-
-        def at(f, j, shift=0):
-            return src[s, f, pl.ds(PITCH * j + 8 + 8 * r + shift, 8), :]
-
-        for j in range(8):
-            gi = ghost_idx + 4 * j
+    for j in range(8):
+        gi = ghost_idx + 4 * j
+        whole = [halves(src[s, f, pl.ds(PITCH * j + 8, 32), :]) for f in range(5)]
+        zz = jnp.dot(
+            jnp.concatenate(whole, axis=0), mat[...], preferred_element_type=jnp.float32
+        )
+        for r in range(4):
+            rows = pl.ds(8 * r, 8)
+
+            def at(f, shift=0, jump=0):
+                return src[s, f, pl.ds(PITCH * (j + jump) + 8 + 8 * r + shift, 8), :]
 
             def field(f):
-                q = at(f, j)
-                xm, xp = at(f, j, -1), at(f, j, 1)
-                up = at(f, j + 1) if j < 7 else layer[py, f, rows, :]
-                dn = at(f, j - 1) if j > 0 else layer[py, f, rows, :]
+                q = at(f)
+                xm, xp = at(f, -1), at(f, 1)
+                up = at(f, 0, 1) if j < 7 else layer[py, f, rows, :]
+                dn = at(f, 0, -1) if j > 0 else layer[py, f, rows, :]
                 g = pick(layer[pz, f, rows, :], gi)
                 yp = pltpu.roll(jnp.where(low, up, q), 96, 1)
                 ym = pltpu.roll(jnp.where(high, dn, q), 32, 1)
-                zp = jnp.where(z31, g, pltpu.roll(q, 127, 1))
-                zm = jnp.where(z0, g, pltpu.roll(q, 1, 1))
+                k = 32 * f + 8 * r
+                zp = jnp.where(z31, g, zz[k : k + 8, :128])
+                zm = jnp.where(z0, g, zz[k : k + 8, 128:])
                 lin = (
                     CENTRE * q
                     + X_UP * xp
@@ -145,7 +164,7 @@
 def body_one(
     plan, n_grp, n_sfc, own_old, own_new, own_crs, nbr, flux_map, fine, coarse, mig, cnew, tab2, *scr
 ):
-    q0, q1, out, c0, c1, cl, l0, l1, inbox, stage, reg, rinbox, rstage, edge, tail, tmp, tab, dsem, ssem, rsem = scr
+    q0, q1, out, c0, c1, cl, l0, l1, inbox, stage, reg, rinbox, rstage, edge, tail, tmp, tab, mat, dsem, ssem, rsem = scr
     devices = n_grp * n_sfc
     me = lax.axis_index("grp") * n_sfc + lax.axis_index("sfc")
 
@@ -169,37 +188,24 @@
         copy.start()
         return copy
 
-    loads = []
-    for j in range(8):
-        rows, cols = pl.ds(PITCH * j + 8, 32), pl.ds(128 * j, 128)
-        loads.append(
-            pltpu.make_async_copy(coarse.at[:, :, :, cols], c0.at[:, :, rows, :], dsem.at[j])
-        )
-    for j in range(8):
-        rows, cols = pl.ds(PITCH * j + 8, 32), pl.ds(128 * j, 128)
-        loads.append(
-            pltpu.make_async_copy(fine.at[:, :, :, cols], q0.at[:, :, rows, :], dsem.at[8 + j])
-        )
-    for copy in loads:
-        copy.start()
-    rest_of_tables = fill_tables(
-        plan, me, own_old, own_new, own_crs, nbr, flux_map, tab, tab2
-    )
     barrier = pltpu.get_barrier_semaphore()
     for shift in shifts:
         pl.semaphore_signal(barrier, inc=1, device_id=peer(shift), device_id_type=MESH)
-    pl.semaphore_wait(barrier, len(shifts))
-    for copy in loads[:8]:
-        copy.wait()
+    loads = []
+    for src, dst, k in ((fine, q0, 0), (coarse, c0, 8)):
+        for j in range(8):
+            rows, cols = pl.ds(PITCH * j + 8, 32), pl.ds(128 * j, 128)
+            loads.append(
+                pltpu.make_async_copy(src.at[:, :, :, cols], dst.at[:, :, rows, :], dsem.at[k + j])
+            )
+    for copy in loads:
+        copy.start()
+    set_z_shift(mat)
+    place_tables, late_tables = fill_tables(
+        plan, me, own_old, own_new, own_crs, nbr, flux_map, tab, tab2
+    )
     count, ccount = tab[40], tab[41]
     at_start, at_end = tab[42] == 1, tab[43] == 1
-
-    for f in range(5):
-        edge[0, f] = x_row(c0, jnp.clip(ccount - 1, 0, CAP - 1), f, 31)
-        edge[1, f] = x_row(c0, 0, f, 0)
-    edges = [send(edge.at[0], edge.at[2], 1), send(edge.at[1], edge.at[3], -1)]
-    for copy in loads[8:]:
-        copy.wait()
 
     def layers_of(src, layer):
         def one(s, _):
@@ -264,10 +270,19 @@
 
         lax.fori_loop(0, OLD, one, 0)
 
+    for copy in loads[:8]:
+        copy.wait()
     layers_of(q0, l0)
+    pl.semaphore_wait(barrier, len(shifts))
     ghosts = exchange(l0, 0)
-
-    rest_of_tables()
+    for copy in loads[8:]:
+        copy.wait()
+    for f in range(5):
+        edge[0, f] = x_row(c0, jnp.clip(ccount - 1, 0, CAP - 1), f, 31)
+        edge[1, f] = x_row(c0, 0, f, 0)
+    edges = [send(edge.at[0], edge.at[2], 1), send(edge.at[1], edge.at[3], -1)]
+
+    place_tables()
     arrive(ghosts, l0, 0)
     x_ghosts(q0, l0)
 
@@ -275,7 +290,7 @@
         def emit(r, j, f, v):
             q1[s, f, pl.ds(PITCH * j + 8 + 8 * r, 8), :] = v
 
-        step(q0, s, l0, tab[10 + s], tab[20 + s], emit)
+        step(q0, s, l0, tab[10 + s], tab[20 + s], mat, emit)
         return 0
 
     lax.fori_loop(0, OLD, fine_one, 0)
@@ -324,11 +339,8 @@
         def emit(r, j, f, v):
             out[s, f, pl.ds(8 * r, 8), pl.ds(128 * j, 128)] = v
 
-        step(q1, s, l1, tab[10 + s], tab[20 + s], emit)
-        return 0
-
-    lax.fori_loop(0, 2, fine_two, 0)
-    moves = [send(out.at[pl.ds(0, 2)], mig.at[pl.ds(12, 2)], -1)]
+        step(q1, s, l1, tab[10 + s], tab[20 + s], mat, emit)
+        return 0
 
     def tail_two(i, _):
         s = jnp.clip(count - 2 + i, 0, OLD - 1)
@@ -336,11 +348,16 @@
         def emit(r, j, f, v):
             tail[i, f, pl.ds(8 * r, 8), pl.ds(128 * j, 128)] = v
 
-        step(q1, s, l1, tab[10 + s], tab[20 + s], emit)
-        return 0
-
-    lax.fori_loop(0, 2, tail_two, 0)
-    moves.append(send(tail, mig.at[pl.ds(10, 2)], 1))
+        step(q1, s, l1, tab[10 + s], tab[20 + s], mat, emit)
+        return 0
+
+    moves = []
+    for i in range(2):
+        lax.fori_loop(i, i + 1, fine_two, 0)
+        moves.append(send(out.at[pl.ds(i, 1)], mig.at[pl.ds(12 + i, 1)], -1))
+        lax.fori_loop(i, i + 1, tail_two, 0)
+        moves.append(send(tail.at[pl.ds(i, 1)], mig.at[pl.ds(10 + i, 1)], 1))
+    late_tables()
     lax.fori_loop(2, 6, fine_two, 0)
     stores = [pltpu.make_async_copy(out.at[pl.ds(0, 6)], mig.at[pl.ds(0, 6)], dsem.at[8])]
     stores[0].start()
@@ -373,7 +390,7 @@
         def emit(r, j, f, v):
             c1[s, f, pl.ds(32 * j + 8 * r, 8), :] = v
 
-        step(c0, s, cl, s, s, emit)
+        step(c0, s, cl, s, s, mat, emit)
         return 0
 
     lax.fori_loop(0, CAP, coarse_step, 0)
@@ -566,37 +583,48 @@
         tab2[n] = jnp.where(p < new[1], jnp.clip(src, 0, OLD + 3), -1)
         return 0
 
-    def rest():
+    def place():
         lax.fori_loop(0, OLD, one_patch, 0)
+
+    def late():
         lax.fori_loop(0, 2 * CAP, one_face, 0)
         lax.fori_loop(0, NEW, one_row, 0)
         tab2[NEW] = crs[1] - crs[0]
 
-    return rest
-
-
-def few_cuts(coarse_owner, owner_old, reflux):
-    total = owner_old.shape[0]
-    ids = jnp.arange(total, dtype=jnp.int32)
-
-    def near(k):
-        edge = owner_old[0] - 1 if k < 0 else owner_old[-1] + 1
-        fill = jnp.full((1,), edge, jnp.int32)
-        if k < 0:
-            return jnp.concatenate([fill, owner_old[:-1]])
-        return jnp.concatenate([owner_old[1:], fill])
-
-    first, last = near(-1) != owner_old, near(1) != owner_old
-    cut = ids % 8
+    return place, late
+
+
+def cuts_body(own_old, own_crs, flux_map, wide_out, target_rows):
+    owner = own_old[...]
+    lane = lane_ids()
+    for j in range(8):
+        target_rows[pl.ds(j, 1), :] = flux_map[pl.ds(0, 1), pl.ds(128 * j, 128)]
+    target = target_rows[...]
+
+    def moved(lane_shift, row_shift, edge):
+        turned = pltpu.roll(owner, lane_shift, 1)
+        return jnp.where(lane == edge, pltpu.roll(turned, row_shift, 0), turned)
+
+    first, last = moved(1, 1, 0) != owner, moved(127, 7, 127) != owner
+    cut = lane % 8
     wide = first & (cut >= 2) & (cut <= 6)
-    target = reflux[:, 0]
-    coarse_ids = jnp.arange(coarse_owner.shape[0], dtype=jnp.int32)
-    onto = jnp.sum(
-        jnp.where(coarse_ids[:, None] == target[None, :], coarse_owner[:, None], 0), axis=0
-    )
-    away = jnp.where(target >= 0, onto - owner_old, 0)
+    spot = jnp.maximum(target, 0) % 128
+    onto = [pick(jnp.broadcast_to(own_crs[pl.ds(k, 1), :], (8, 128)), spot) for k in range(2)]
+    away = jnp.where(target >= 0, jnp.where(target < 128, onto[0], onto[1]) - owner, 0)
     far = (jnp.abs(away) > 2) | ((away == 2) & ~last) | ((away == -2) & ~first)
-    return ~jnp.any(wide | far)
+    wide_out[0] = jnp.max(jnp.where(wide | far, 1, 0))
+
+
+def cuts(owners, flux_map):
+    vmem = pl.BlockSpec(memory_space=pltpu.VMEM)
+    return pl.pallas_call(
+        cuts_body,
+        name="cuts",
+        out_shape=jax.ShapeDtypeStruct((1,), jnp.int32),
+        in_specs=[vmem] * 3,
+        out_specs=pl.BlockSpec(memory_space=pltpu.SMEM),
+        scratch_shapes=[pltpu.VMEM((8, 128), jnp.int32)],
+    )(owners[0], owners[2], flux_map)
 
 
 def stage_one(plan, number, n_grp, n_sfc, owners, nbr, flux_map, fine, coarse):
@@ -634,6 +662,7 @@
             pltpu.VMEM((2, 5, 32, 1024), f32),
             pltpu.VMEM((5, 8, 128), f32),
             pltpu.SMEM((128,), jnp.int32),
+            pltpu.VMEM((256, 256), jnp.bfloat16),
             pltpu.SemaphoreType.DMA((16,)),
             pltpu.SemaphoreType.DMA((24,)),
             pltpu.SemaphoreType.DMA((24,)),
@@ -674,7 +703,7 @@
         owners = (owner_old.reshape(8, -1), owner_new.reshape(8, -1), coarse_owner.reshape(2, -1))
         args = (owners, nbr.T, reflux.T, fine_old, coarse_state)
         mig, cnew, tab = lax.cond(
-            few_cuts(coarse_owner, owner_old, reflux),
+            cuts(owners, reflux.T)[0] == 0,
             functools.partial(stage_one, common, 0, n_grp, n_sfc),
             functools.partial(stage_one, general, 1, n_grp, n_sfc),
             *args,

time: 81.2 us -> 69.1 us (0.85)
  Pallas kernels: 72.6 us -> 67.1 us
  local copies, waits for them, and re-layouts: 2.9 us -> 0 us
  other arithmetic: 2.3 us -> 0 us
  between operations: 2.76 us -> 1.45 us
    pallas_call x1, Pallas kernels: 64.5 us -> 57.7 us  [stage_one(): pl.pallas_call(functools.partial(body_one, plan, n_grp, n_sfc), name='adv...]
    slice x3 -> x0, local copies, waits for them, and re-layouts: 2.9 us -> none  [the longest x1 1.34 us: near(): edge = owner_old[0] - 1 if k < 0 else owner_old[-1] + 1]
    pallas_call x0 -> x1, Pallas kernels: none -> 1.56 us  [cuts(): pl.pallas_call(cuts_body, name='cuts', out_shape=jax.ShapeDtypeStruct((1,...]
    reduce_or x1 -> x0, other arithmetic: 1.4 us -> none  [few_cuts(): return ~jnp.any(wide | far)]
    reduce_sum x1 -> x0, other arithmetic: 0.89 us -> none  [few_cuts(): jnp.sum(jnp.where(coarse_ids[:, None] == target[None, :], coarse_owner[:,...]
where the time goes in v3:
time: 69.1 us; the launch traced here: 68.8 us
  Pallas kernels  67.1 us (97%)
  between operations  1.45 us (2%)
    pallas_call x1, Pallas kernels, stage_one(): pl.pallas_call(functools.partial(body_one, plan, n_grp, n_sfc), name='adv...  57.7 us
    pallas_call x1, Pallas kernels, stage_two(): pl.pallas_call(body_two, name='place_patches', out_shape=(jax.ShapeDtypeS...  7.83 us
    pallas_call x1, Pallas kernels, cuts(): pl.pallas_call(cuts_body, name='cuts', out_shape=jax.ShapeDtypeStruct((1,...  1.56 us

profile of v3, /device:TPU:0, one launch (start us, length us, event | category | flops | bytes accessed | tf_op | source)
XLA Modules:
  0.0 68.8 jit_solution(10732039822545628082)
XLA Ops:
  0.6 1.6 %cuts.1 = s32[1]{0:T(128)} custom-call(s32[8,128]{1,0:T(8,128)} %bitcast.11, s32[2,128]{1,0:T(2,128)} %bitcast.16, s32[3,1024]{1,0:T(4,128)} %bitcast.6), custom_call_target="tpu_custom_call" | custom-call | tf_op jit(solution)/shard_map/cuts/pallas_call | solution.py:620
  2.8 57.9 %conditional.1 = ((f32[14,5,32,1024]{3,2,1,0:T(8,128)}, f32[3,5,32,1024]{3,2,1,0:T(8,128)S(1)}, s32[16]{0:T(128)S(1)})) conditional(s32[]{:T(128)} %bitcast.3, (s32[8,128]{1,0:T(8,128)}, s32[8,128]{1,0:T(8,128)}, s32[2,128]{1,0:T(2,128)}, s32[6,1024]{1,0:T(8,128)}, s32[3,1024]{1,0:T(4,128)}, /*index=5*/f32[10,5,32,1024]{3,2,1,0:T(8,128)}, ...), branch_computations={%region_0.0_spmd, %region_1.0_spmd} | conditional | bytes 8 | solution.py:705
  3.0 57.7 %advance_level.3 = (f32[14,5,32,1024]{3,2,1,0:T(8,128)}, f32[3,5,32,1024]{3,2,1,0:T(8,128)S(1)}, s32[16]{0:T(128)S(1)}) custom-call(s32[8,128]{1,0:T(8,128)} %get-tuple-element.35.own_old, s32[8,128]{1,0:T(8,128)} %get-tuple-element.36.own_new, s32[2,128]{1,0:T(2,128)} %get-tuple-element.37.own_crs, s32[6,1024]{1,0:T(8,128)} %get-tuple-element.38.nbr, ...), custom_call_target="tpu_custom_call" | custom-call | tf_op jit(solution)/shard_map/cond/branch_1_fun/advance_level/pallas_call | solution.py:637
  60.8 7.8 %place_patches.1 = (f32[3,5,32,1024]{3,2,1,0:T(8,128)}, f32[14,5,32,1024]{3,2,1,0:T(8,128)}) custom-call(s32[16]{0:T(128)S(1)} %get-tuple-element.47.tab, f32[14,5,32,1024]{3,2,1,0:T(8,128)} %get-tuple-element.48.mig, f32[3,5,32,1024]{3,2,1,0:T(8,128)S(1)} %get-tuple-element.49.cnew), custom_call_target="tpu_custom_call" | custom-call | tf_op jit(solution)/shard_map/place_patches/pallas_call | solution.py:679

commit v4 on v3

--- a/solution.py
+++ b/solution.py
@@ -192,11 +192,14 @@
     for shift in shifts:
         pl.semaphore_signal(barrier, inc=1, device_id=peer(shift), device_id_type=MESH)
     loads = []
-    for src, dst, k in ((fine, q0, 0), (coarse, c0, 8)):
+    for src, dst, k, first, n in ((fine, q0, 0, 0, 3), (fine, q0, 8, 3, 7), (coarse, c0, 16, 0, CAP)):
         for j in range(8):
             rows, cols = pl.ds(PITCH * j + 8, 32), pl.ds(128 * j, 128)
+            some = pl.ds(first, n)
             loads.append(
-                pltpu.make_async_copy(src.at[:, :, :, cols], dst.at[:, :, rows, :], dsem.at[k + j])
+                pltpu.make_async_copy(
+                    src.at[some, :, :, cols], dst.at[some, :, rows, :], dsem.at[k + j]
+                )
             )
     for copy in loads:
         copy.start()
@@ -207,7 +210,7 @@
     count, ccount = tab[40], tab[41]
     at_start, at_end = tab[42] == 1, tab[43] == 1
 
-    def layers_of(src, layer):
+    def layers_of(src, layer, first=0, end=OLD):
         def one(s, _):
             make_layers(src, s, layer)
             inner_low = tab[30 + s] == 1
@@ -217,7 +220,7 @@
                 )
             return 0
 
-        lax.fori_loop(0, OLD, one, 0)
+        lax.fori_loop(first, end, one, 0)
 
     def exchange(layer, part):
         copies = []
@@ -272,10 +275,13 @@
 
     for copy in loads[:8]:
         copy.wait()
-    layers_of(q0, l0)
+    layers_of(q0, l0, 0, 3)
+    for copy in loads[8:16]:
+        copy.wait()
+    layers_of(q0, l0, 3, OLD)
     pl.semaphore_wait(barrier, len(shifts))
     ghosts = exchange(l0, 0)
-    for copy in loads[8:]:
+    for copy in loads[16:]:
         copy.wait()
     for f in range(5):
         edge[0, f] = x_row(c0, jnp.clip(ccount - 1, 0, CAP - 1), f, 31)
@@ -663,7 +669,7 @@
             pltpu.VMEM((5, 8, 128), f32),
             pltpu.SMEM((128,), jnp.int32),
             pltpu.VMEM((256, 256), jnp.bfloat16),
-            pltpu.SemaphoreType.DMA((16,)),
+            pltpu.SemaphoreType.DMA((24,)),
             pltpu.SemaphoreType.DMA((24,)),
             pltpu.SemaphoreType.DMA((24,)),
         ],

time: 69.1 us -> 68.3 us (0.988)
  Pallas kernels: 67.1 us -> 66.3 us
where the time goes in v4:
time: 68.3 us; the launch traced here: 67.9 us
  Pallas kernels  66.3 us (97%)
  between operations  1.45 us (2%)
    pallas_call x1, Pallas kernels, stage_one(): pl.pallas_call(functools.partial(body_one, plan, n_grp, n_sfc), name='adv...  57.2 us
    pallas_call x1, Pallas kernels, stage_two(): pl.pallas_call(body_two, name='place_patches', out_shape=(jax.ShapeDtypeS...  7.49 us
    pallas_call x1, Pallas kernels, cuts(): pl.pallas_call(cuts_body, name='cuts', out_shape=jax.ShapeDtypeStruct((1,...  1.56 us

profile of v4, /device:TPU:0, one launch (start us, length us, event | category | flops | bytes accessed | tf_op | source)
XLA Modules:
  0.0 67.9 jit_solution(10198572264187506247)
XLA Ops:
  0.6 1.6 %cuts.1 = s32[1]{0:T(128)} custom-call(s32[8,128]{1,0:T(8,128)} %bitcast.11, s32[2,128]{1,0:T(2,128)} %bitcast.16, s32[3,1024]{1,0:T(4,128)} %bitcast.6), custom_call_target="tpu_custom_call" | custom-call | tf_op jit(solution)/shard_map/cuts/pallas_call | solution.py:626
  2.8 57.4 %conditional.1 = ((f32[14,5,32,1024]{3,2,1,0:T(8,128)}, f32[3,5,32,1024]{3,2,1,0:T(8,128)S(1)}, s32[16]{0:T(128)S(1)})) conditional(s32[]{:T(128)} %bitcast.3, (s32[8,128]{1,0:T(8,128)}, s32[8,128]{1,0:T(8,128)}, s32[2,128]{1,0:T(2,128)}, s32[6,1024]{1,0:T(8,128)}, s32[3,1024]{1,0:T(4,128)}, /*index=5*/f32[10,5,32,1024]{3,2,1,0:T(8,128)}, ...), branch_computations={%region_0.0_spmd, %region_1.0_spmd} | conditional | bytes 8 | solution.py:711
  3.0 57.2 %advance_level.3 = (f32[14,5,32,1024]{3,2,1,0:T(8,128)}, f32[3,5,32,1024]{3,2,1,0:T(8,128)S(1)}, s32[16]{0:T(128)S(1)}) custom-call(s32[8,128]{1,0:T(8,128)} %get-tuple-element.35.own_old, s32[8,128]{1,0:T(8,128)} %get-tuple-element.36.own_new, s32[2,128]{1,0:T(2,128)} %get-tuple-element.37.own_crs, s32[6,1024]{1,0:T(8,128)} %get-tuple-element.38.nbr, ...), custom_call_target="tpu_custom_call" | custom-call | tf_op jit(solution)/shard_map/cond/branch_1_fun/advance_level/pallas_call | solution.py:643
  60.3 7.5 %place_patches.1 = (f32[3,5,32,1024]{3,2,1,0:T(8,128)}, f32[14,5,32,1024]{3,2,1,0:T(8,128)}) custom-call(s32[16]{0:T(128)S(1)} %get-tuple-element.47.tab, f32[14,5,32,1024]{3,2,1,0:T(8,128)} %get-tuple-element.48.mig, f32[3,5,32,1024]{3,2,1,0:T(8,128)S(1)} %get-tuple-element.49.cnew), custom_call_target="tpu_custom_call" | custom-call | tf_op jit(solution)/shard_map/place_patches/pallas_call | solution.py:685
